TPU v7x, 32 devices: a whole 2x2x4 slice. The times are simulated.
32 devices in a mesh: cuts: 16 (over z, y, core), coil: 2 (over x).
Axes of the slice: x: 2, y: 2, z: 4, core: 2. Of those that a mesh axis runs over, the one named last changes fastest.
Arguments:
- radial: bfloat16 [4, 16, 2, 49152], P('coil', 'cuts'), may hold values from -6 to 6
- band_start: int32 [48, 8], replicated, may hold values from 0 to 240
- row_offset: int32 [48, 8, 128], replicated, may hold values from 0 to 12
- col_offset: int32 [48, 8, 128], replicated, may hold values from 0 to 252
- weight_rows: bfloat16 [48, 8, 4, 128], replicated, may hold values from 0.099609375 to 1
- weight_cols: bfloat16 [48, 8, 4, 128], replicated, may hold values from 0.099609375 to 1
- coil_maps: bfloat16 [4, 2, 256, 128], P('coil', None, 'cuts'), may hold values from -3 to 3
- low_part: float32 [256, 2, 48, 128], P(('cuts', 'coil')), may hold values from -24 to 24
- sparse_part: float32 [256, 2, 48, 128], P(('cuts', 'coil')), may hold values from -6 to 6
- basis_old: float32 [96, 32], replicated, may hold values from -6 to 6
- thresholds: float32 [48], replicated, may hold values from 0.2 to 1.5
Outputs:
- low_new: float32 [256, 2, 48, 128], P(('cuts', 'coil'))
- sparse_new: float32 [256, 2, 48, 128], P(('cuts', 'coil'))
- basis_new: float32 [96, 32], replicated
All inputs are finite; a program needn't handle non-finite values.
Results may differ from a plain program's by a relative error of at most 0.0019.
Values may be sent and summed in bfloat16 or wider, within the bound.
A program may use at most 128 MiB of HBM per device.

v0:
```python
import functools
import math

import jax
import jax.numpy as jnp
import numpy as np
from jax import lax
from jax.experimental import pallas as pl
from jax.experimental.pallas import tpu as pltpu
from jax.sharding import PartitionSpec as P

POWER = 2
KY = 256
KX = 256
BAND = 16
LANES = 128

PRECISE = lax.Precision.HIGHEST
MESH = pl.DeviceIdType.MESH
VMEM = pl.BlockSpec(memory_space=pltpu.VMEM)
HBM = pl.BlockSpec(memory_space=pltpu.HBM)


def phase_pair(product, length):
    angles = 2.0 * math.pi / length * np.remainder(product, length).astype(np.float64)
    return np.cos(angles), np.sin(angles)


def slice_table(slice_count):
    ids = np.arange(slice_count) - slice_count // 2
    cosine, sine = phase_pair(ids[:, None] * ids[None, :], slice_count)
    coeffs = np.stack([np.stack([cosine, -sine], -1), np.stack([sine, cosine], -1)], 1)
    return (coeffs / math.sqrt(slice_count)).astype(jnp.bfloat16)


def row_tables(row_count):
    grid_row = np.arange(KY) - KY // 2
    image_row = np.arange(row_count) - row_count // 2
    cosine, sine = phase_pair(grid_row[:, None] * image_row[None, :], KY)
    coeffs = np.stack([np.concatenate([cosine, sine], 1), np.concatenate([-sine, cosine], 1)], 0)
    return (coeffs / math.sqrt(KY)).astype(jnp.bfloat16).astype(np.float32)


def column_table(image_cols):
    grid_col = np.arange(KX) - KX // 2
    image_col = np.arange(image_cols) - image_cols // 2
    cosine, sine = phase_pair(grid_col[:, None] * image_col[None, :], KX)
    coeffs = np.concatenate(
        [np.concatenate([cosine, sine], 1), np.concatenate([-sine, cosine], 1)], 0
    )
    return (coeffs / math.sqrt(KX)).astype(jnp.bfloat16)


def time_tables(frames):
    ids = np.arange(frames)
    cosine, sine = phase_pair(ids[:, None] * ids[None, :], frames)
    forward = np.concatenate(
        [np.concatenate([cosine, sine], 1), np.concatenate([-sine, cosine], 1)], 0
    )
    inverse = np.concatenate(
        [np.concatenate([cosine, -sine], 1), np.concatenate([sine, cosine], 1)], 0
    )
    scaling = 1.0 / math.sqrt(frames)
    return (forward * scaling).astype(np.float32), (inverse * scaling).astype(np.float32)


def run(make, low, high, action):
    def step(d, carry):
        action(make(d))
        return carry

    lax.fori_loop(low, high, step, 0)


def start(copy):
    copy.start()


def wait(copy):
    copy.wait()


def tap_weights(distance, taps):
    value = jnp.where(distance == 0, taps[0], 0.0)
    for t in range(1, len(taps)):
        value = jnp.where(distance == t, taps[t], value)
    return value


def precise_dot(a, b, dims):
    return lax.dot_general(
        a, b, (dims, ((), ())), precision=PRECISE, preferred_element_type=jnp.float32
    )


def orthonormal_rows(powered):
    rank, columns = powered.shape
    inner = precise_dot(powered, powered, ((1,), (1,)))
    joint = jnp.concatenate([powered, inner], 1)
    row_ids = lax.broadcasted_iota(jnp.int32, joint.shape, 0)
    scale = jnp.ones_like(joint)
    batch = math.gcd(rank, 8)
    for first in range(0, rank, batch):
        at = columns + first
        wide = [
            jnp.broadcast_to(joint[:, at + i : at + i + 1], joint.shape) for i in range(batch)
        ]
        for i in range(batch):
            j = first + i
            inverse = 1.0 / wide[i][j : j + 1]
            factor = jnp.where(row_ids > j, wide[i] * inverse, 0.0)
            for k in range(i + 1, batch):
                wide[k] = wide[k] - factor * wide[k][j : j + 1]
            joint = joint - factor * joint[j : j + 1]
            scale = jnp.where(row_ids == j, inverse, scale)
    return joint[:, :columns] * jnp.sqrt(scale[:, :columns])


def fused_kernel(
    n_cuts, n_coil, inner_cuts, group, direct,
    start_ref, tab_hbm, rowtab_hbm, coltab_hbm, basis_hbm, radial_ref, maps_ref,
    roff_hbm, coff_hbm, wrow_hbm, wcol_hbm, low_hbm, sparse_hbm,
    pieces, basis_out,
    tab_ref, rowtab_ref, coltab_ref, basis_ref, rbuf, sbuf, samples, maps_all, roff_ref, coff_ref, wrow_ref, wcol_ref, low_ref, sparse_ref,
    gridded, rtab, spectra, back, gram_own, gram_in, part_own, part_in, sum_own, gram_all,
    send1, recv1, send2, recv2, send3, recv3, send4, recv4, send5, recv5, send6, recv6,
    send7, recv7, local_sem, own_sem,
):
    me_c = lax.axis_index("cuts")
    me_h = lax.axis_index("coil")
    n = n_cuts * n_coil
    flat = me_c * n_coil + me_h
    steps = samples.shape[0]
    group_len = samples.shape[2]
    channels = samples.shape[1]
    coils = channels // 2
    coils_here = coils // n_coil
    here = roff_ref.shape[0]
    blocks = roff_ref.shape[1]
    block_len = roff_ref.shape[2]
    rows = maps_all.shape[2]
    cols = maps_all.shape[3]
    rows_here = low_ref.shape[0]
    columns = low_ref.shape[1]
    frames = columns // 2
    chunk = rbuf.shape[-1]
    barrier = pltpu.get_barrier_semaphore()
    stride = next(k for k in range(3 * n // 8, n + 2) if math.gcd(k, n) == 1)

    def place(d):
        target = lax.rem(flat + d * stride, n)
        return target // n_coil, lax.rem(target, n_coil)

    def greet(d, carry):
        pl.semaphore_signal(barrier, inc=1, device_id=place(d), device_id_type=MESH)
        return carry

    lax.fori_loop(1, n, greet, 0)

    mine = pl.ds(me_h * here, here)
    local_copies = [
        pltpu.make_async_copy(source, target, local_sem.at[i])
        for i, (source, target) in enumerate(
            [
                (roff_hbm.at[mine], roff_ref),
                (coff_hbm.at[mine], coff_ref),
                (wrow_hbm.at[mine], wrow_ref),
                (wcol_hbm.at[mine], wcol_ref),
                (rowtab_hbm, rowtab_ref),
                (coltab_hbm, coltab_ref),
                (basis_hbm, basis_ref),
                (low_hbm, low_ref),
                (sparse_hbm, sparse_ref),
            ]
        )
    ]
    tab_copy = pltpu.make_async_copy(tab_hbm, tab_ref, local_sem.at[len(local_copies)])
    own_at = pl.ds(pl.multiple_of(me_c * chunk, LANES), chunk)
    my_coils = pl.ds(me_h * coils_here, coils_here)

    def own_part(g, t_c, t_h):
        first = pl.multiple_of((t_h * steps + g) * group_len + t_c * chunk, LANES)
        return radial_ref.at[:, 0, :, pl.ds(first, chunk)]

    def own_first(g):
        return pltpu.make_async_copy(
            own_part(g, me_c, me_h), rbuf.at[g, me_c, me_h], own_sem.at[g]
        )

    def first(i):
        g = i // (n - 1)
        d = 1 + lax.rem(i, n - 1)
        t_c, t_h = place(d)
        return pltpu.make_async_remote_copy(
            src_ref=own_part(g, t_c, t_h),
            dst_ref=rbuf.at[g, me_c, me_h],
            send_sem=send1.at[i],
            recv_sem=recv1.at[i],
            device_id=(t_c, t_h),
            device_id_type=MESH,
        )

    def own_second(g):
        return pltpu.make_async_copy(
            sbuf.at[g, me_c], samples.at[g, :, own_at], own_sem.at[steps + g]
        )

    def second(i):
        g = i // (n_cuts - 1)
        t_c = lax.rem(me_c + 1 + lax.rem(i, n_cuts - 1), n_cuts)
        return pltpu.make_async_remote_copy(
            src_ref=sbuf.at[g, t_c],
            dst_ref=samples.at[g, :, own_at],
            send_sem=send2.at[i],
            recv_sem=recv2.at[i],
            device_id=(t_c, me_h),
            device_id_type=MESH,
        )

    def maps_copy(d):
        return pltpu.make_async_remote_copy(
            src_ref=maps_ref,
            dst_ref=maps_all.at[my_coils],
            send_sem=send3.at[d],
            recv_sem=recv3.at[d],
            device_id=(me_c, lax.rem(me_h + d, n_coil)),
            device_id_type=MESH,
        )

    def back_copy(i):
        g = i // (n_coil - 1)
        t_h = lax.rem(me_h + 1 + lax.rem(i, n_coil - 1), n_coil)
        return pltpu.make_async_remote_copy(
            src_ref=back.at[g, pl.ds(t_h * rows_here, rows_here)],
            dst_ref=pieces.at[me_h, g],
            send_sem=send4.at[i],
            recv_sem=recv4.at[i],
            device_id=(me_c, t_h),
            device_id_type=MESH,
        )

    my_maps = maps_all.at[my_coils] if direct else maps_all
    own_maps = pltpu.make_async_copy(maps_ref, my_maps, own_sem.at[2 * steps])
    tab_copy.start()
    if direct:
        run(own_first, 0, steps, start)
        own_maps.start()
        pl.semaphore_wait(barrier, n - 1)
        run(first, 0, min(2, steps) * (n - 1), start)
        run(maps_copy, 1, n_coil, start)
    else:
        pl.semaphore_wait(barrier, n - 1)
        own_maps.start()
        local_copies += [
            pltpu.make_async_copy(
                radial_ref.at[:, pl.ds(g * group_len, group_len)], samples.at[g], own_sem.at[g]
            )
            for g in range(steps)
        ]
    for copy in local_copies:
        copy.start()
    tab_copy.wait()

    def mix(g):
        own_first(g).wait()
        run(first, g * (n - 1), (g + 1) * (n - 1), wait)
        pl.when(g + 2 < steps)(
            lambda: run(first, (g + 2) * (n - 1), (g + 3) * (n - 1), start)
        )
        gathered = rbuf[g].reshape(tab_ref.shape[1], chunk)
        mixed = jnp.dot(tab_ref[...], gathered, preferred_element_type=jnp.float32)
        sbuf[g] = mixed.reshape(n_cuts, channels, chunk).astype(jnp.bfloat16)
        run(second, g * (n_cuts - 1), (g + 1) * (n_cuts - 1), start)
        own_second(g).start()

    if direct:
        for g in range(min(2, steps)):
            mix(g)
        run(maps_copy, 1, n_coil, wait)
    own_maps.wait()
    for copy in local_copies:
        copy.wait()

    tile = 16
    packed = jnp.bfloat16

    def spread(row):
        return jnp.broadcast_to(row.astype(jnp.float32), (tile, block_len)).astype(packed)[None]

    col_ids = (
        lax.broadcasted_iota(jnp.int32, (KX, block_len), 0)
        .astype(jnp.float32)
        .astype(packed)
        .reshape(KX // tile, tile, block_len)
    )
    row_ids = lax.broadcasted_iota(jnp.int32, (BAND, block_len), 0)

    def images_of(g, carry):
        if direct:
            own_second(g).wait()
            run(second, g * (n_cuts - 1), (g + 1) * (n_cuts - 1), wait)

        def frame(f, inner_carry):
            at_frame = g * group + f
            for b in range(blocks):
                taps = wrow_ref[at_frame, b].astype(jnp.float32)
                row_w = tap_weights(
                    row_ids - roff_ref[at_frame, b : b + 1, :],
                    [taps[t : t + 1] for t in range(taps.shape[0])],
                )
                taps = wcol_ref[at_frame, b]
                col_w = tap_weights(
                    col_ids - spread(coff_ref[at_frame, b : b + 1, :]),
                    [spread(taps[t : t + 1]) for t in range(taps.shape[0])],
                ).astype(packed).reshape(KX, block_len)
                lane = pl.multiple_of((f * blocks + b) * block_len, LANES)
                data = samples[g, :, pl.ds(lane, block_len)].astype(jnp.float32)
                weighted = jnp.concatenate(
                    [data[i : i + 1] * row_w for i in range(channels)], 0
                ).astype(jnp.bfloat16)
                grid_part = lax.dot_general(
                    weighted, col_w, (((1,), (1,)), ((), ())), preferred_element_type=jnp.float32
                ).astype(jnp.bfloat16)
                size = 2 * BAND
                for c in range(coils):
                    gridded[b * size : (b + 1) * size, c * KX : (c + 1) * KX] = grid_part[
                        c * size : (c + 1) * size
                    ]
                first_row = start_ref[b, me_h * here + at_frame]
                for p in range(2):
                    rtab[b * size + p * BAND : b * size + (p + 1) * BAND, :] = rowtab_ref[
                        p, pl.ds(first_row, BAND), :
                    ].astype(jnp.bfloat16)
            spec = lax.dot_general(
                rtab[...], gridded[...], (((0,), (0,)), ((), ())),
                preferred_element_type=jnp.float32,
            ).astype(jnp.bfloat16)
            for c in range(coils):
                for q in range(2):
                    spectra[
                        pl.ds(pl.multiple_of((f * coils + c) * rows, rows), rows),
                        q * KX : (q + 1) * KX,
                    ] = spec[q * rows : (q + 1) * rows, c * KX : (c + 1) * KX]
            return inner_carry

        lax.fori_loop(0, group, frame, 0)
        images = jnp.dot(spectra[...], coltab_ref[...], preferred_element_type=jnp.float32)
        for f in range(group):
            real = 0.0
            imag = 0.0
            for c in range(coils):
                at = (f * coils + c) * rows
                image_re = images[at : at + rows, :cols]
                image_im = images[at : at + rows, cols:]
                sens_re = maps_all[c, 0].astype(jnp.float32)
                sens_im = maps_all[c, 1].astype(jnp.float32)
                real = real + (image_re * sens_re + image_im * sens_im)
                imag = imag + (image_im * sens_re - image_re * sens_im)
            back[g, :, 0, f, :] = real
            back[g, :, 1, f, :] = imag
        run(back_copy, g * (n_coil - 1), (g + 1) * (n_coil - 1), start)
        if direct:
            pl.when(g + 2 < steps)(lambda: mix(g + 2))
        return carry

    lax.fori_loop(0, steps, images_of, 0)
    for g in range(steps):
        pieces[me_h, g] = back[g, pl.ds(me_h * rows_here, rows_here)]
    run(back_copy, 0, steps * (n_coil - 1), wait)

    gram = jnp.zeros((columns, columns), jnp.float32)
    for r in range(rows_here):
        part = centre(pieces, low_ref, sparse_ref, r)[1]
        gram = gram + precise_dot(part, part, ((1,), (1,)))

    plane = inner_cuts * n_coil
    outer_cuts = n_cuts // inner_cuts
    me_plane = lax.rem(me_c, inner_cuts) * n_coil + me_h
    me_outer = me_c // inner_cuts
    piece = columns // plane

    def plane_place(d):
        target = lax.rem(me_plane + d, plane)
        return target, (me_outer * inner_cuts + target // n_coil, lax.rem(target, n_coil))

    def scatter(d):
        target, device = plane_place(d)
        return pltpu.make_async_remote_copy(
            src_ref=gram_own.at[target],
            dst_ref=gram_in.at[me_plane],
            send_sem=send5.at[d],
            recv_sem=recv5.at[d],
            device_id=device,
            device_id_type=MESH,
        )

    def across(d):
        target = lax.rem(me_outer + d, outer_cuts)
        return pltpu.make_async_remote_copy(
            src_ref=part_own,
            dst_ref=part_in.at[me_outer],
            send_sem=send6.at[d],
            recv_sem=recv6.at[d],
            device_id=(target * inner_cuts + lax.rem(me_c, inner_cuts), me_h),
            device_id_type=MESH,
        )

    def gather(d):
        target, device = plane_place(d)
        return pltpu.make_async_remote_copy(
            src_ref=sum_own,
            dst_ref=gram_all.at[me_plane],
            send_sem=send7.at[d],
            recv_sem=recv7.at[d],
            device_id=device,
            device_id_type=MESH,
        )

    for i in range(plane):
        gram_own[i] = gram[i * piece : (i + 1) * piece]
    run(scatter, 1, plane, start)
    gram_in[me_plane] = gram_own[me_plane]
    run(scatter, 1, plane, wait)
    value = gram_in[0]
    for i in range(1, plane):
        value = value + gram_in[i]
    part_own[...] = value
    run(across, 1, outer_cuts, start)
    part_in[me_outer] = value
    run(across, 1, outer_cuts, wait)
    value = part_in[0]
    for i in range(1, outer_cuts):
        value = value + part_in[i]
    sum_own[...] = value
    run(gather, 1, plane, start)
    gram_all[me_plane] = value
    run(gather, 1, plane, wait)
    gram = jnp.concatenate([gram_all[i] for i in range(plane)], 0)

    basis = basis_ref[...]
    for repeat in range(POWER):
        basis = orthonormal_rows(precise_dot(basis, gram, ((1,), (0,))))
    basis_out[...] = basis


def centre(pieces, low_ref, sparse_ref, r):
    n_coil, steps = pieces.shape[:2]
    back = jnp.concatenate(
        [pieces[h, g, r, p] for p in range(2) for h in range(n_coil) for g in range(steps)], 0
    )
    sparse = sparse_ref[r]
    merged = low_ref[r] + sparse - back
    return merged, merged - sparse


def finish_kernel(
    pieces_hbm, low_hbm, sparse_hbm, basis_hbm, level_hbm, fwd_hbm, inv_hbm,
    low_out, sparse_out, basis_out,
    pieces, low_ref, sparse_ref, basis_ref, level_ref, fwd_ref, inv_ref, low_new, sparse_new,
    load_sem, store_sem,
):
    frames = level_ref.shape[1]
    rows_here = low_ref.shape[0]
    loads = [
        pltpu.make_async_copy(source, target, load_sem.at[i])
        for i, (source, target) in enumerate(
            [
                (basis_hbm, basis_ref),
                (level_hbm, level_ref),
                (pieces_hbm, pieces),
                (low_hbm, low_ref),
                (sparse_hbm, sparse_ref),
                (fwd_hbm, fwd_ref),
                (inv_hbm, inv_ref),
            ]
        )
    ]
    for copy in loads:
        copy.start()
    for copy in loads[:2]:
        copy.wait()
    basis = basis_ref[...]
    project = precise_dot(basis, basis, ((0,), (0,)))
    same = lax.broadcasted_iota(jnp.int32, (frames, frames), 0) == lax.broadcasted_iota(
        jnp.int32, (frames, frames), 1
    )
    levels = jnp.sum(jnp.where(same, level_ref[...], 0.0), axis=1, keepdims=True)
    for copy in loads[2:]:
        copy.wait()
    stores = [pltpu.make_async_copy(basis_ref, basis_out, store_sem.at[2 * rows_here])]
    stores[0].start()
    for r in range(rows_here):
        merged, centred = centre(pieces, low_ref, sparse_ref, r)
        low = precise_dot(project, centred, ((1,), (0,)))
        low_new[r] = low
        stores.append(pltpu.make_async_copy(low_new.at[r], low_out.at[r], store_sem.at[2 * r]))
        stores[-1].start()
        spectrum = precise_dot(fwd_ref[...], merged - low, ((1,), (0,)))
        real, imag = spectrum[:frames], spectrum[frames:]
        modulus = jnp.sqrt(real * real + imag * imag)
        factor = jnp.maximum(modulus - levels, 0.0) / jnp.maximum(modulus, levels)
        shrunk = jnp.concatenate([real * factor, imag * factor], 0)
        sparse_new[r] = precise_dot(inv_ref[...], shrunk, ((1,), (0,)))
        stores.append(
            pltpu.make_async_copy(sparse_new.at[r], sparse_out.at[r], store_sem.at[2 * r + 1])
        )
        stores[-1].start()
    for copy in stores:
        copy.wait()


def local(
    radial,
    band_start,
    row_offset,
    col_offset,
    weight_rows,
    weight_cols,
    coil_maps,
    low_part,
    sparse_part,
    basis_old,
    thresholds,
):
    n_cuts = lax.axis_size("cuts")
    n_coil = lax.axis_size("coil")
    n = n_cuts * n_coil
    coils = radial.shape[0] * n_coil
    frames, blocks = band_start.shape
    block_len = row_offset.shape[2]
    taps = weight_rows.shape[2]
    rows_here, _, _, cols = low_part.shape
    rows = coil_maps.shape[2]
    columns = 2 * frames
    rank = basis_old.shape[1]
    here = frames // n_coil
    group = 8 if here % 8 == 0 else here
    steps = here // group
    share = radial.shape[3] // n_coil
    group_len = share // steps
    direct = n_coil > 1 and group_len % (n_cuts * LANES) == 0
    tab = slice_table(n_cuts)
    if direct:
        chunk = group_len // n_cuts
        wide = np.einsum("zskp,ij->ziskjp", tab.astype(np.float32), np.eye(coils))
        wide = jnp.asarray(wide.reshape(n_cuts * coils * 2, n_cuts * coils * 2), jnp.bfloat16)
        data, maps = radial, coil_maps
    else:
        chunk = LANES
        wide = jnp.zeros((8, LANES), jnp.bfloat16)
        by_half = lax.all_to_all(radial, "coil", split_axis=3, concat_axis=0, tiled=True)
        mixed = jnp.einsum(
            "zskp,ikpn->zisn",
            jnp.asarray(tab),
            lax.all_to_all(by_half, "cuts", split_axis=3, concat_axis=1, tiled=True),
            preferred_element_type=jnp.float32,
        )
        by_slice = lax.all_to_all(
            mixed.astype(jnp.bfloat16), "cuts", split_axis=0, concat_axis=3, tiled=True
        )
        data = by_slice.reshape(2 * coils, share)
        maps = lax.all_gather(coil_maps, "coil", axis=0, tiled=True)
    inner_cuts = 4 if n_cuts % 4 == 0 and columns % (4 * n_coil) == 0 else 1
    plane = inner_cuts * n_coil
    outer = n_cuts // inner_cuts
    piece = columns // plane
    flat = (rows_here, columns, cols)
    rowtab = jnp.asarray(row_tables(rows))
    coltab = jnp.asarray(column_table(cols))
    low_flat = low_part.reshape(flat)
    sparse_flat = sparse_part.reshape(flat)
    forward, inverse = time_tables(frames)
    dma = pltpu.SemaphoreType.DMA
    bf16, f32 = jnp.bfloat16, jnp.float32
    exchanged = (steps, n_cuts) if direct else (1, 1)
    smem = pl.BlockSpec(memory_space=pltpu.SMEM)
    hbm = HBM
    pieces, basis = pl.pallas_call(
        functools.partial(fused_kernel, n_cuts, n_coil, inner_cuts, group, direct),
        out_shape=(
            jax.ShapeDtypeStruct((n_coil, steps, rows_here, 2, group, cols), f32),
            jax.ShapeDtypeStruct((rank, columns), f32),
        ),
        in_specs=[smem] + [hbm] * 12,
        out_specs=(VMEM, VMEM),
        scratch_shapes=[
            pltpu.VMEM(wide.shape, bf16),
            pltpu.VMEM(rowtab.shape, f32),
            pltpu.VMEM(coltab.shape, bf16),
            pltpu.VMEM((rank, columns), f32),
            pltpu.VMEM(exchanged + (n_coil, radial.shape[0], 2, chunk), bf16),
            pltpu.VMEM(exchanged + (2 * coils, chunk), bf16),
            pltpu.VMEM((steps, 2 * coils, group_len), bf16),
            pltpu.VMEM((coils,) + coil_maps.shape[1:], bf16),
            pltpu.VMEM((here, blocks, block_len), jnp.int32),
            pltpu.VMEM((here, blocks, block_len), jnp.int32),
            pltpu.VMEM((here, blocks, taps, block_len), bf16),
            pltpu.VMEM((here, blocks, taps, block_len), bf16),
            pltpu.VMEM(flat, f32),
            pltpu.VMEM(flat, f32),
            pltpu.VMEM((blocks * 2 * BAND, coils * KX), bf16),
            pltpu.VMEM((blocks * 2 * BAND, 2 * rows), bf16),
            pltpu.VMEM((group * coils * rows, 2 * KX), bf16),
            pltpu.VMEM((steps, rows, 2, group, cols), f32),
            pltpu.VMEM((plane, piece, columns), f32),
            pltpu.VMEM((plane, piece, columns), f32),
            pltpu.VMEM((piece, columns), f32),
            pltpu.VMEM((outer, piece, columns), f32),
            pltpu.VMEM((piece, columns), f32),
            pltpu.VMEM((plane, piece, columns), f32),
            dma((steps * n,)),
            dma((steps * n,)),
            dma((steps * n_cuts,)),
            dma((steps * n_cuts,)),
            dma((n_coil,)),
            dma((n_coil,)),
            dma((steps * n_coil,)),
            dma((steps * n_coil,)),
            dma((plane,)),
            dma((plane,)),
            dma((outer,)),
            dma((outer,)),
            dma((plane,)),
            dma((plane,)),
            dma((10,)),
            dma((2 * steps + 1,)),
        ],
        compiler_params=pltpu.CompilerParams(
            collective_id=0, has_side_effects=True
        ),
        name="back_and_basis",
    )(
        band_start.T, wide, rowtab, coltab, basis_old.T, data, maps,
        row_offset, col_offset, weight_rows, weight_cols, low_flat, sparse_flat,
    )
    low_new, sparse_new, basis = pl.pallas_call(
        finish_kernel,
        out_shape=(
            jax.ShapeDtypeStruct(flat, f32),
            jax.ShapeDtypeStruct(flat, f32),
            jax.ShapeDtypeStruct((rank, columns), f32),
        ),
        in_specs=[HBM] * 7,
        out_specs=(HBM, HBM, HBM),
        scratch_shapes=[
            pltpu.VMEM(pieces.shape, f32),
            pltpu.VMEM(flat, f32),
            pltpu.VMEM(flat, f32),
            pltpu.VMEM((rank, columns), f32),
            pltpu.VMEM((1, frames), f32),
            pltpu.VMEM((columns, columns), f32),
            pltpu.VMEM((columns, columns), f32),
            pltpu.VMEM(flat, f32),
            pltpu.VMEM(flat, f32),
            dma((7,)),
            dma((2 * rows_here + 1,)),
        ],
        name="finish",
    )(
        pieces, low_flat, sparse_flat, basis, thresholds.reshape(1, frames),
        jnp.asarray(forward), jnp.asarray(inverse),
    )
    return low_new.reshape(low_part.shape), sparse_new.reshape(low_part.shape), basis.T


def solution(mesh):
    placed = (
        P("coil", "cuts", None, None),
        P(),
        P(),
        P(),
        P(),
        P(),
        P("coil", None, "cuts", None),
        P(("cuts", "coil"), None, None, None),
        P(("cuts", "coil"), None, None, None),
        P(),
        P(),
    )
    return jax.shard_map(
        local,
        mesh=mesh,
        in_specs=placed,
        out_specs=(
            P(("cuts", "coil"), None, None, None),
            P(("cuts", "coil"), None, None, None),
            P(),
        ),
        check_vma=False,
    )
```

profile of v0, /device:TPU:0, one launch (start us, length us, event | category | flops | bytes accessed | tf_op | source)
XLA Modules:
  0.0 64.8 jit_solution(1807169610531162383)
XLA Ops:
  0.6 59.3 %back_and_basis.1 = (f32[2,3,8,2,8,128]{5,4,3,2,1,0:T(8,128)}, f32[32,96]{1,0:T(8,128)}) custom-call(s32[8,48]{1,0:T(8,128)} %bitcast.13, bf16[128,128]{1,0:T(8,128)(2,1)} %constant.10.clone.tab_hbm, f32[2,256,32]{2,1,0:T(8,128)} %constant.11.clone.rowtab_hbm, bf16[512,256]{1,0:T(8,128)(2,1)} %constant.12.clone.coltab_hbm, f32[32,96]{1,0:T(8,128)} %bitcast.12, ...), custom_call_target="tpu_custom_call" | custom-call | tf_op jit(solution)/shard_map/back_and_basis/pallas_call | solution.py:578
  60.0 4.8 %finish.1 = (f32[8,96,128]{2,1,0:T(8,128)}, f32[8,96,128]{2,1,0:T(8,128)}, f32[32,96]{1,0:T(8,128)}) custom-call(f32[2,3,8,2,8,128]{5,4,3,2,1,0:T(8,128)} %get-tuple-element.8.pieces_hbm, f32[8,96,128]{2,1,0:T(8,128)} %bitcast.9, f32[8,96,128]{2,1,0:T(8,128)} %bitcast.11, f32[32,96]{1,0:T(8,128)} %get-tuple-element.9.basis_hbm, f32[1,48]{1,0:T(1,128)} %bitcast.14, ...), custom_call_target="tpu_custom_call" | custom-call | tf_op jit(solution)/shard_map/finish/pallas_call | solution.py:636
where the time goes:
time: 65.1 us; the launch traced here: 64.8 us
  Pallas kernels  64.1 us (98%)
    pallas_call x1, Pallas kernels, local(): pl.pallas_call(functools.partial(fused_kernel, n_cuts, n_coil, inner_cuts...  59.3 us
    pallas_call x1, Pallas kernels, local(): pl.pallas_call(finish_kernel, out_shape=(jax.ShapeDtypeStruct(flat, f32),...  4.8 us

commit v1 on v0

--- a/solution.py
+++ b/solution.py
@@ -33,11 +33,11 @@
     return (coeffs / math.sqrt(slice_count)).astype(jnp.bfloat16)
 
 
-def row_tables(row_count):
+def row_table(row_count):
     grid_row = np.arange(KY) - KY // 2
     image_row = np.arange(row_count) - row_count // 2
     cosine, sine = phase_pair(grid_row[:, None] * image_row[None, :], KY)
-    coeffs = np.stack([np.concatenate([cosine, sine], 1), np.concatenate([-sine, cosine], 1)], 0)
+    coeffs = np.concatenate([cosine, sine], 1)
     return (coeffs / math.sqrt(KY)).astype(jnp.bfloat16).astype(np.float32)
 
 
@@ -122,7 +122,7 @@
     roff_hbm, coff_hbm, wrow_hbm, wcol_hbm, low_hbm, sparse_hbm,
     pieces, basis_out,
     tab_ref, rowtab_ref, coltab_ref, basis_ref, rbuf, sbuf, samples, maps_all, roff_ref, coff_ref, wrow_ref, wcol_ref, low_ref, sparse_ref,
-    gridded, rtab, spectra, back, gram_own, gram_in, part_own, part_in, sum_own, gram_all,
+    col_all, factors, band_w, rtab, spectra, back, gram_own, gram_in, part_own, part_in, sum_own, gram_all,
     send1, recv1, send2, recv2, send3, recv3, send4, recv4, send5, recv5, send6, recv6,
     send7, recv7, local_sem, own_sem,
 ):
@@ -241,46 +241,37 @@
 
     my_maps = maps_all.at[my_coils] if direct else maps_all
     own_maps = pltpu.make_async_copy(maps_ref, my_maps, own_sem.at[2 * steps])
+    for copy in local_copies[:5]:
+        copy.start()
     tab_copy.start()
+    own_maps.start()
     if direct:
         run(own_first, 0, steps, start)
-        own_maps.start()
-        pl.semaphore_wait(barrier, n - 1)
-        run(first, 0, min(2, steps) * (n - 1), start)
-        run(maps_copy, 1, n_coil, start)
     else:
-        pl.semaphore_wait(barrier, n - 1)
-        own_maps.start()
         local_copies += [
             pltpu.make_async_copy(
                 radial_ref.at[:, pl.ds(g * group_len, group_len)], samples.at[g], own_sem.at[g]
             )
             for g in range(steps)
         ]
-    for copy in local_copies:
+        pl.semaphore_wait(barrier, n - 1)
+    late_copies = local_copies[5:] + ([] if direct else [tab_copy])
+    for copy in local_copies[5:]:
         copy.start()
-    tab_copy.wait()
+    for copy in local_copies[:5]:
+        copy.wait()
 
     def mix(g):
         own_first(g).wait()
         run(first, g * (n - 1), (g + 1) * (n - 1), wait)
-        pl.when(g + 2 < steps)(
-            lambda: run(first, (g + 2) * (n - 1), (g + 3) * (n - 1), start)
-        )
+        if g == 0:
+            tab_copy.wait()
         gathered = rbuf[g].reshape(tab_ref.shape[1], chunk)
         mixed = jnp.dot(tab_ref[...], gathered, preferred_element_type=jnp.float32)
         sbuf[g] = mixed.reshape(n_cuts, channels, chunk).astype(jnp.bfloat16)
         run(second, g * (n_cuts - 1), (g + 1) * (n_cuts - 1), start)
         own_second(g).start()
 
-    if direct:
-        for g in range(min(2, steps)):
-            mix(g)
-        run(maps_copy, 1, n_coil, wait)
-    own_maps.wait()
-    for copy in local_copies:
-        copy.wait()
-
     tile = 16
     packed = jnp.bfloat16
 
@@ -295,6 +286,52 @@
     )
     row_ids = lax.broadcasted_iota(jnp.int32, (BAND, block_len), 0)
 
+    def weights(f, carry):
+        for b in range(blocks):
+            lanes = slice(b * block_len, (b + 1) * block_len)
+            band = slice(b * BAND, (b + 1) * BAND)
+            taps = wrow_ref[f, b].astype(jnp.float32)
+            band_w[band, lanes] = tap_weights(
+                row_ids - roff_ref[f, b : b + 1, :],
+                [taps[t : t + 1] for t in range(taps.shape[0])],
+            ).astype(packed)
+            first_row = start_ref[b, me_h * here + f]
+            rtab[band, :] = rowtab_ref[pl.ds(first_row, BAND), :].astype(packed)
+            taps = wcol_ref[f, b]
+            col_all[f, :, lanes] = (
+                tap_weights(
+                    col_ids - spread(coff_ref[f, b : b + 1, :]),
+                    [spread(taps[t : t + 1]) for t in range(taps.shape[0])],
+                )
+                .astype(packed)
+                .reshape(KX, block_len)
+            )
+        factors[f] = lax.dot_general(
+            rtab[...], band_w[...], (((0,), (0,)), ((), ())), preferred_element_type=jnp.float32
+        )
+        return carry
+
+    def ahead(low, high):
+        lax.fori_loop(low, high, weights, 0)
+
+    band_w[...] = jnp.zeros_like(band_w)
+    if direct:
+        marks = [here // 6] + [here // 2 + i * (here - here // 2) // (steps + 1) for i in range(steps)] + [here]
+        ahead(0, marks[0])
+        pl.semaphore_wait(barrier, n - 1)
+        run(first, 0, steps * (n - 1), start)
+        run(maps_copy, 1, n_coil, start)
+        for g in range(steps):
+            ahead(marks[g], marks[g + 1])
+            mix(g)
+        ahead(marks[steps], marks[steps + 1])
+        run(maps_copy, 1, n_coil, wait)
+    else:
+        ahead(0, here)
+    own_maps.wait()
+    for copy in late_copies:
+        copy.wait()
+
     def images_of(g, carry):
         if direct:
             own_second(g).wait()
@@ -302,45 +339,29 @@
 
         def frame(f, inner_carry):
             at_frame = g * group + f
+            parts = []
             for b in range(blocks):
-                taps = wrow_ref[at_frame, b].astype(jnp.float32)
-                row_w = tap_weights(
-                    row_ids - roff_ref[at_frame, b : b + 1, :],
-                    [taps[t : t + 1] for t in range(taps.shape[0])],
-                )
-                taps = wcol_ref[at_frame, b]
-                col_w = tap_weights(
-                    col_ids - spread(coff_ref[at_frame, b : b + 1, :]),
-                    [spread(taps[t : t + 1]) for t in range(taps.shape[0])],
-                ).astype(packed).reshape(KX, block_len)
+                lanes = slice(b * block_len, (b + 1) * block_len)
+                cosine = factors[at_frame, :rows, lanes]
+                sine = factors[at_frame, rows:, lanes]
                 lane = pl.multiple_of((f * blocks + b) * block_len, LANES)
                 data = samples[g, :, pl.ds(lane, block_len)].astype(jnp.float32)
-                weighted = jnp.concatenate(
-                    [data[i : i + 1] * row_w for i in range(channels)], 0
-                ).astype(jnp.bfloat16)
-                grid_part = lax.dot_general(
-                    weighted, col_w, (((1,), (1,)), ((), ())), preferred_element_type=jnp.float32
-                ).astype(jnp.bfloat16)
-                size = 2 * BAND
+                turned = []
                 for c in range(coils):
-                    gridded[b * size : (b + 1) * size, c * KX : (c + 1) * KX] = grid_part[
-                        c * size : (c + 1) * size
-                    ]
-                first_row = start_ref[b, me_h * here + at_frame]
-                for p in range(2):
-                    rtab[b * size + p * BAND : b * size + (p + 1) * BAND, :] = rowtab_ref[
-                        p, pl.ds(first_row, BAND), :
-                    ].astype(jnp.bfloat16)
+                    real = data[2 * c : 2 * c + 1]
+                    imag = data[2 * c + 1 : 2 * c + 2]
+                    turned += [real * cosine - imag * sine, real * sine + imag * cosine]
+                parts.append(jnp.concatenate(turned, 0).astype(packed))
             spec = lax.dot_general(
-                rtab[...], gridded[...], (((0,), (0,)), ((), ())),
+                jnp.concatenate(parts, 1), col_all[at_frame], (((1,), (1,)), ((), ())),
                 preferred_element_type=jnp.float32,
-            ).astype(jnp.bfloat16)
+            ).astype(packed)
             for c in range(coils):
                 for q in range(2):
                     spectra[
                         pl.ds(pl.multiple_of((f * coils + c) * rows, rows), rows),
                         q * KX : (q + 1) * KX,
-                    ] = spec[q * rows : (q + 1) * rows, c * KX : (c + 1) * KX]
+                    ] = spec[(2 * c + q) * rows : (2 * c + q + 1) * rows]
             return inner_carry
 
         lax.fori_loop(0, group, frame, 0)
@@ -359,8 +380,6 @@
             back[g, :, 0, f, :] = real
             back[g, :, 1, f, :] = imag
         run(back_copy, g * (n_coil - 1), (g + 1) * (n_coil - 1), start)
-        if direct:
-            pl.when(g + 2 < steps)(lambda: mix(g + 2))
         return carry
 
     lax.fori_loop(0, steps, images_of, 0)
@@ -565,7 +584,7 @@
     outer = n_cuts // inner_cuts
     piece = columns // plane
     flat = (rows_here, columns, cols)
-    rowtab = jnp.asarray(row_tables(rows))
+    rowtab = jnp.asarray(row_table(rows))
     coltab = jnp.asarray(column_table(cols))
     low_flat = low_part.reshape(flat)
     sparse_flat = sparse_part.reshape(flat)
@@ -598,8 +617,10 @@
             pltpu.VMEM((here, blocks, taps, block_len), bf16),
             pltpu.VMEM(flat, f32),
             pltpu.VMEM(flat, f32),
-            pltpu.VMEM((blocks * 2 * BAND, coils * KX), bf16),
-            pltpu.VMEM((blocks * 2 * BAND, 2 * rows), bf16),
+            pltpu.VMEM((here, KX, blocks * block_len), bf16),
+            pltpu.VMEM((here, 2 * rows, blocks * block_len), f32),
+            pltpu.VMEM((blocks * BAND, blocks * block_len), bf16),
+            pltpu.VMEM((blocks * BAND, 2 * rows), bf16),
             pltpu.VMEM((group * coils * rows, 2 * KX), bf16),
             pltpu.VMEM((steps, rows, 2, group, cols), f32),
             pltpu.VMEM((plane, piece, columns), f32),

time: 65.1 us -> 59.9 us (0.920)
  Pallas kernels: 64.1 us -> 58.9 us
    pallas_call x1, Pallas kernels: 59.3 us -> 54.1 us  [local(): pl.pallas_call(functools.partial(fused_kernel, n_cuts, n_coil, inner_cuts...]
where the time goes in v1:
time: 59.9 us; the launch traced here: 59.6 us
  Pallas kernels  58.9 us (98%)
  between operations  0.64 us (1%)
    pallas_call x1, Pallas kernels, local(): pl.pallas_call(functools.partial(fused_kernel, n_cuts, n_coil, inner_cuts...  54.1 us
    pallas_call x1, Pallas kernels, local(): pl.pallas_call(finish_kernel, out_shape=(jax.ShapeDtypeStruct(flat, f32),...  4.8 us

profile of v1, /device:TPU:0, one launch (start us, length us, event | category | flops | bytes accessed | tf_op | source)
XLA Modules:
  0.0 59.6 jit_solution(6323949570997857707)
XLA Ops:
  0.6 54.1 %back_and_basis.1 = (f32[2,3,8,2,8,128]{5,4,3,2,1,0:T(8,128)}, f32[32,96]{1,0:T(8,128)}) custom-call(s32[8,48]{1,0:T(8,128)} %bitcast.13, bf16[128,128]{1,0:T(8,128)(2,1)} %constant.10.clone.tab_hbm, f32[256,32]{1,0:T(8,128)} %constant.11.clone.rowtab_hbm, bf16[512,256]{1,0:T(8,128)(2,1)} %constant.12.clone.coltab_hbm, f32[32,96]{1,0:T(8,128)} %bitcast.12, ...), custom_call_target="tpu_custom_call" | custom-call | tf_op jit(solution)/shard_map/back_and_basis/pallas_call | solution.py:597
  54.8 4.8 %finish.1 = (f32[8,96,128]{2,1,0:T(8,128)}, f32[8,96,128]{2,1,0:T(8,128)}, f32[32,96]{1,0:T(8,128)}) custom-call(f32[2,3,8,2,8,128]{5,4,3,2,1,0:T(8,128)} %get-tuple-element.8.pieces_hbm, f32[8,96,128]{2,1,0:T(8,128)} %bitcast.9, f32[8,96,128]{2,1,0:T(8,128)} %bitcast.11, f32[32,96]{1,0:T(8,128)} %get-tuple-element.9.basis_hbm, f32[1,48]{1,0:T(1,128)} %bitcast.14, ...), custom_call_target="tpu_custom_call" | custom-call | tf_op jit(solution)/shard_map/finish/pallas_call | solution.py:657

commit v2 on v1

--- a/solution.py
+++ b/solution.py
@@ -14,6 +14,7 @@
 KX = 256
 BAND = 16
 LANES = 128
+PAIR = 2
 
 PRECISE = lax.Precision.HIGHEST
 MESH = pl.DeviceIdType.MESH
@@ -64,12 +65,17 @@
     return (forward * scaling).astype(np.float32), (inverse * scaling).astype(np.float32)
 
 
-def run(make, low, high, action):
-    def step(d, carry):
-        action(make(d))
+def run(make, low, high, action, width=1):
+    def step(i, carry):
+        for j in range(width):
+            action(make(low + i * width + j))
         return carry
 
-    lax.fori_loop(low, high, step, 0)
+    count = (high - low) // width if width > 1 else high - low
+    lax.fori_loop(0, count, step, 0)
+    if width > 1:
+        for d in range(low + count * width, high):
+            action(make(d))
 
 
 def start(copy):
@@ -78,6 +84,19 @@
 
 def wait(copy):
     copy.wait()
+
+
+LAST = ((1,), (1,))
+INNER = ((1,), (0,))
+
+
+def halves(values):
+    high = values.astype(jnp.bfloat16)
+    return high, (values - high.astype(jnp.float32)).astype(jnp.bfloat16)
+
+
+def narrow_dot(a, b, dims):
+    return lax.dot_general(a, b, (dims, ((), ())), preferred_element_type=jnp.float32)
 
 
 def tap_weights(distance, taps):
@@ -118,13 +137,14 @@
 
 def fused_kernel(
     n_cuts, n_coil, inner_cuts, group, direct,
-    start_ref, tab_hbm, rowtab_hbm, coltab_hbm, basis_hbm, radial_ref, maps_ref,
-    roff_hbm, coff_hbm, wrow_hbm, wcol_hbm, low_hbm, sparse_hbm,
-    pieces, basis_out,
-    tab_ref, rowtab_ref, coltab_ref, basis_ref, rbuf, sbuf, samples, maps_all, roff_ref, coff_ref, wrow_ref, wcol_ref, low_ref, sparse_ref,
-    col_all, factors, band_w, rtab, spectra, back, gram_own, gram_in, part_own, part_in, sum_own, gram_all,
+    start_hbm, tab_hbm, rowtab_hbm, coltab_hbm, basis_hbm, radial_ref, maps_ref,
+    roff_hbm, coff_hbm, wrow_hbm, wcol_hbm, low_hbm, sparse_hbm, fwd_hbm,
+    high_out, low_out, turned_out, basis_out,
+    pieces, fwd_ref, high, low, whole, turned,
+    start_ref, tab_ref, rowtab_ref, coltab_ref, basis_ref, rbuf, sbuf, samples, maps_all, roff_ref, coff_ref, wrow_ref, wcol_ref, low_ref, sparse_ref,
+    wave, col_all, factors, band_w, rtab, spectra, back, gram_own, gram_in, part_own, part_in, sum_own, gram_all,
     send1, recv1, send2, recv2, send3, recv3, send4, recv4, send5, recv5, send6, recv6,
-    send7, recv7, local_sem, own_sem,
+    send7, recv7, local_sem, out_sem, own_sem,
 ):
     me_c = lax.axis_index("cuts")
     me_h = lax.axis_index("coil")
@@ -167,10 +187,12 @@
                 (wrow_hbm.at[mine], wrow_ref),
                 (wcol_hbm.at[mine], wcol_ref),
                 (rowtab_hbm, rowtab_ref),
+                (start_hbm, start_ref),
                 (coltab_hbm, coltab_ref),
                 (basis_hbm, basis_ref),
                 (low_hbm, low_ref),
                 (sparse_hbm, sparse_ref),
+                (fwd_hbm, fwd_ref),
             ]
         )
     ]
@@ -187,15 +209,13 @@
             own_part(g, me_c, me_h), rbuf.at[g, me_c, me_h], own_sem.at[g]
         )
 
-    def first(i):
-        g = i // (n - 1)
-        d = 1 + lax.rem(i, n - 1)
+    def first(g, d):
         t_c, t_h = place(d)
         return pltpu.make_async_remote_copy(
             src_ref=own_part(g, t_c, t_h),
             dst_ref=rbuf.at[g, me_c, me_h],
-            send_sem=send1.at[i],
-            recv_sem=recv1.at[i],
+            send_sem=send1.at[g * n + d],
+            recv_sem=recv1.at[g * n + d],
             device_id=(t_c, t_h),
             device_id_type=MESH,
         )
@@ -205,14 +225,13 @@
             sbuf.at[g, me_c], samples.at[g, :, own_at], own_sem.at[steps + g]
         )
 
-    def second(i):
-        g = i // (n_cuts - 1)
-        t_c = lax.rem(me_c + 1 + lax.rem(i, n_cuts - 1), n_cuts)
+    def second(g, d):
+        t_c = lax.rem(me_c + d, n_cuts)
         return pltpu.make_async_remote_copy(
             src_ref=sbuf.at[g, t_c],
             dst_ref=samples.at[g, :, own_at],
-            send_sem=send2.at[i],
-            recv_sem=recv2.at[i],
+            send_sem=send2.at[g * n_cuts + d],
+            recv_sem=recv2.at[g * n_cuts + d],
             device_id=(t_c, me_h),
             device_id_type=MESH,
         )
@@ -241,7 +260,7 @@
 
     my_maps = maps_all.at[my_coils] if direct else maps_all
     own_maps = pltpu.make_async_copy(maps_ref, my_maps, own_sem.at[2 * steps])
-    for copy in local_copies[:5]:
+    for copy in local_copies[:6]:
         copy.start()
     tab_copy.start()
     own_maps.start()
@@ -255,21 +274,21 @@
             for g in range(steps)
         ]
         pl.semaphore_wait(barrier, n - 1)
-    late_copies = local_copies[5:] + ([] if direct else [tab_copy])
-    for copy in local_copies[5:]:
+    late_copies = local_copies[6:] + ([] if direct else [tab_copy])
+    for copy in local_copies[6:]:
         copy.start()
-    for copy in local_copies[:5]:
+    for copy in local_copies[:6]:
         copy.wait()
 
     def mix(g):
         own_first(g).wait()
-        run(first, g * (n - 1), (g + 1) * (n - 1), wait)
+        run(functools.partial(first, g), 1, n, wait)
         if g == 0:
             tab_copy.wait()
         gathered = rbuf[g].reshape(tab_ref.shape[1], chunk)
         mixed = jnp.dot(tab_ref[...], gathered, preferred_element_type=jnp.float32)
         sbuf[g] = mixed.reshape(n_cuts, channels, chunk).astype(jnp.bfloat16)
-        run(second, g * (n_cuts - 1), (g + 1) * (n_cuts - 1), start)
+        run(functools.partial(second, g), 1, n_cuts, start, 5)
         own_second(g).start()
 
     tile = 16
@@ -278,34 +297,37 @@
     def spread(row):
         return jnp.broadcast_to(row.astype(jnp.float32), (tile, block_len)).astype(packed)[None]
 
-    col_ids = (
-        lax.broadcasted_iota(jnp.int32, (KX, block_len), 0)
-        .astype(jnp.float32)
-        .astype(packed)
-        .reshape(KX // tile, tile, block_len)
-    )
-    row_ids = lax.broadcasted_iota(jnp.int32, (BAND, block_len), 0)
+    ids = lax.broadcasted_iota(jnp.int32, (1, tile, block_len), 1).astype(jnp.float32).astype(packed)
+    none = jnp.zeros_like(ids)
 
     def weights(f, carry):
+        offsets = coff_ref[f]
+        places = (offsets // tile).astype(jnp.float32)
+        inside = (offsets % tile).astype(jnp.float32)
+        row_at = roff_ref[f].astype(jnp.float32)
         for b in range(blocks):
             lanes = slice(b * block_len, (b + 1) * block_len)
             band = slice(b * BAND, (b + 1) * BAND)
-            taps = wrow_ref[f, b].astype(jnp.float32)
+            taps = wrow_ref[f, b]
             band_w[band, lanes] = tap_weights(
-                row_ids - roff_ref[f, b : b + 1, :],
-                [taps[t : t + 1] for t in range(taps.shape[0])],
-            ).astype(packed)
+                ids - spread(row_at[b : b + 1]), [spread(taps[t : t + 1]) for t in range(taps.shape[0])]
+            ).astype(packed).reshape(BAND, block_len)
             first_row = start_ref[b, me_h * here + f]
             rtab[band, :] = rowtab_ref[pl.ds(first_row, BAND), :].astype(packed)
             taps = wcol_ref[f, b]
-            col_all[f, :, lanes] = (
-                tap_weights(
-                    col_ids - spread(coff_ref[f, b : b + 1, :]),
-                    [spread(taps[t : t + 1]) for t in range(taps.shape[0])],
-                )
-                .astype(packed)
-                .reshape(KX, block_len)
-            )
+            taps = [spread(taps[t : t + 1]) for t in range(taps.shape[0])]
+            distance = ids - spread(inside[b : b + 1])
+            first = tap_weights(distance, taps).astype(packed)
+            spill = none
+            for t in range(1, len(taps)):
+                spill = jnp.where(distance == t - tile, taps[t], spill)
+            place = spread(places[b : b + 1])
+            before = None
+            for i in range(KX // tile):
+                hit = place == i
+                value = jnp.where(hit, first, none if before is None else jnp.where(before, spill, none))
+                col_all[f, i * tile : (i + 1) * tile, lanes] = value.reshape(tile, block_len)
+                before = hit
         factors[f] = lax.dot_general(
             rtab[...], band_w[...], (((0,), (0,)), ((), ())), preferred_element_type=jnp.float32
         )
@@ -316,15 +338,17 @@
 
     band_w[...] = jnp.zeros_like(band_w)
     if direct:
-        marks = [here // 6] + [here // 2 + i * (here - here // 2) // (steps + 1) for i in range(steps)] + [here]
+        marks = [here // 6]
+        for i in range(steps):
+            marks.append(here - (here - marks[0]) * 2 * (steps - 1 - i) // (5 * max(1, steps - 1)))
         ahead(0, marks[0])
         pl.semaphore_wait(barrier, n - 1)
-        run(first, 0, steps * (n - 1), start)
+        for g in range(steps):
+            run(functools.partial(first, g), 1, n, start, 4)
         run(maps_copy, 1, n_coil, start)
         for g in range(steps):
             ahead(marks[g], marks[g + 1])
             mix(g)
-        ahead(marks[steps], marks[steps + 1])
         run(maps_copy, 1, n_coil, wait)
     else:
         ahead(0, here)
@@ -335,21 +359,22 @@
     def images_of(g, carry):
         if direct:
             own_second(g).wait()
-            run(second, g * (n_cuts - 1), (g + 1) * (n_cuts - 1), wait)
-
-        def frame(f, inner_carry):
+            run(functools.partial(second, g), 1, n_cuts, wait)
+
+        for i in range(group * blocks):
+            wave[i] = samples[g, :, i * block_len : (i + 1) * block_len].astype(jnp.float32)
+
+        def frame(f):
             at_frame = g * group + f
             parts = []
             for b in range(blocks):
                 lanes = slice(b * block_len, (b + 1) * block_len)
                 cosine = factors[at_frame, :rows, lanes]
                 sine = factors[at_frame, rows:, lanes]
-                lane = pl.multiple_of((f * blocks + b) * block_len, LANES)
-                data = samples[g, :, pl.ds(lane, block_len)].astype(jnp.float32)
                 turned = []
                 for c in range(coils):
-                    real = data[2 * c : 2 * c + 1]
-                    imag = data[2 * c + 1 : 2 * c + 2]
+                    real = wave.at[f * blocks + b][pl.ds(2 * c, rows, stride=0), :]
+                    imag = wave.at[f * blocks + b][pl.ds(2 * c + 1, rows, stride=0), :]
                     turned += [real * cosine - imag * sine, real * sine + imag * cosine]
                 parts.append(jnp.concatenate(turned, 0).astype(packed))
             spec = lax.dot_general(
@@ -362,9 +387,13 @@
                         pl.ds(pl.multiple_of((f * coils + c) * rows, rows), rows),
                         q * KX : (q + 1) * KX,
                     ] = spec[(2 * c + q) * rows : (2 * c + q + 1) * rows]
+
+        def several(i, inner_carry):
+            for j in range(PAIR):
+                frame(i * PAIR + j)
             return inner_carry
 
-        lax.fori_loop(0, group, frame, 0)
+        lax.fori_loop(0, group // PAIR, several, 0)
         images = jnp.dot(spectra[...], coltab_ref[...], preferred_element_type=jnp.float32)
         for f in range(group):
             real = 0.0
@@ -387,10 +416,23 @@
         pieces[me_h, g] = back[g, pl.ds(me_h * rows_here, rows_here)]
     run(back_copy, 0, steps * (n_coil - 1), wait)
 
-    gram = jnp.zeros((columns, columns), jnp.float32)
     for r in range(rows_here):
-        part = centre(pieces, low_ref, sparse_ref, r)[1]
-        gram = gram + precise_dot(part, part, ((1,), (1,)))
+        lanes = slice(r * cols, (r + 1) * cols)
+        part = jnp.concatenate(
+            [
+                pieces[h, g, r, p]
+                for p in range(2)
+                for h in range(n_coil)
+                for g in range(steps)
+            ],
+            0,
+        )
+        sparse = sparse_ref[r]
+        merged = low_ref[r] + sparse - part
+        whole[:, lanes] = merged
+        high[:, lanes], low[:, lanes] = halves(merged - sparse)
+    gram = narrow_dot(high[...], high[...], LAST)
+    gram = gram + narrow_dot(low[...], high[...], LAST) + narrow_dot(high[...], low[...], LAST)
 
     plane = inner_cuts * n_coil
     outer_cuts = n_cuts // inner_cuts
@@ -439,6 +481,15 @@
         gram_own[i] = gram[i * piece : (i + 1) * piece]
     run(scatter, 1, plane, start)
     gram_in[me_plane] = gram_own[me_plane]
+    turned[...] = precise_dot(fwd_ref[...], whole[...], ((1,), (0,)))
+    outputs = [
+        pltpu.make_async_copy(source, target, out_sem.at[i])
+        for i, (source, target) in enumerate(
+            [(high, high_out), (low, low_out), (turned, turned_out)]
+        )
+    ]
+    for copy in outputs:
+        copy.start()
     run(scatter, 1, plane, wait)
     value = gram_in[0]
     for i in range(1, plane):
@@ -460,70 +511,74 @@
     for repeat in range(POWER):
         basis = orthonormal_rows(precise_dot(basis, gram, ((1,), (0,))))
     basis_out[...] = basis
-
-
-def centre(pieces, low_ref, sparse_ref, r):
-    n_coil, steps = pieces.shape[:2]
-    back = jnp.concatenate(
-        [pieces[h, g, r, p] for p in range(2) for h in range(n_coil) for g in range(steps)], 0
-    )
-    sparse = sparse_ref[r]
-    merged = low_ref[r] + sparse - back
-    return merged, merged - sparse
+    for copy in outputs:
+        copy.wait()
 
 
 def finish_kernel(
-    pieces_hbm, low_hbm, sparse_hbm, basis_hbm, level_hbm, fwd_hbm, inv_hbm,
+    basis_hbm, level_hbm, high_hbm, low_hbm, turned_hbm, fwd_hbm, inv_high_hbm, inv_low_hbm,
     low_out, sparse_out, basis_out,
-    pieces, low_ref, sparse_ref, basis_ref, level_ref, fwd_ref, inv_ref, low_new, sparse_new,
-    load_sem, store_sem,
+    basis_ref, level_ref, high_ref, low_ref, turned_ref, fwd_ref, inv_high, inv_low,
+    low_new, sparse_new, load_sem, store_sem,
 ):
     frames = level_ref.shape[1]
-    rows_here = low_ref.shape[0]
+    rows_here, columns, cols = low_new.shape
     loads = [
         pltpu.make_async_copy(source, target, load_sem.at[i])
         for i, (source, target) in enumerate(
             [
                 (basis_hbm, basis_ref),
+                (fwd_hbm, fwd_ref),
                 (level_hbm, level_ref),
-                (pieces_hbm, pieces),
+                (high_hbm, high_ref),
                 (low_hbm, low_ref),
-                (sparse_hbm, sparse_ref),
-                (fwd_hbm, fwd_ref),
-                (inv_hbm, inv_ref),
+                (turned_hbm, turned_ref),
+                (inv_high_hbm, inv_high),
+                (inv_low_hbm, inv_low),
             ]
         )
     ]
     for copy in loads:
         copy.start()
-    for copy in loads[:2]:
-        copy.wait()
-    basis = basis_ref[...]
-    project = precise_dot(basis, basis, ((0,), (0,)))
-    same = lax.broadcasted_iota(jnp.int32, (frames, frames), 0) == lax.broadcasted_iota(
-        jnp.int32, (frames, frames), 1
-    )
-    levels = jnp.sum(jnp.where(same, level_ref[...], 0.0), axis=1, keepdims=True)
-    for copy in loads[2:]:
+    for copy in loads[:3]:
         copy.wait()
     stores = [pltpu.make_async_copy(basis_ref, basis_out, store_sem.at[2 * rows_here])]
     stores[0].start()
-    for r in range(rows_here):
-        merged, centred = centre(pieces, low_ref, sparse_ref, r)
-        low = precise_dot(project, centred, ((1,), (0,)))
-        low_new[r] = low
-        stores.append(pltpu.make_async_copy(low_new.at[r], low_out.at[r], store_sem.at[2 * r]))
-        stores[-1].start()
-        spectrum = precise_dot(fwd_ref[...], merged - low, ((1,), (0,)))
+    basis = basis_ref[...]
+    project = precise_dot(basis, basis, ((0,), (0,)))
+    project = jnp.concatenate([project, precise_dot(fwd_ref[...], project, INNER)], 0)
+    project_high, project_low = halves(project)
+    same = lax.broadcasted_iota(jnp.int32, (frames, frames), 0) == lax.broadcasted_iota(
+        jnp.int32, (frames, frames), 1
+    )
+    levels = jnp.sum(jnp.where(same, level_ref[...], 0.0), axis=1, keepdims=True)
+    for copy in loads[3:]:
+        copy.wait()
+    together = math.gcd(rows_here, 2)
+    for first in range(0, rows_here, together):
+        lanes = slice(first * cols, (first + together) * cols)
+        high = high_ref[:, lanes]
+        both = narrow_dot(project_high, high, INNER) + (
+            narrow_dot(project_low, high, INNER) + narrow_dot(project_high, low_ref[:, lanes], INNER)
+        )
+        spectrum = turned_ref[:, lanes] - both[columns:]
         real, imag = spectrum[:frames], spectrum[frames:]
         modulus = jnp.sqrt(real * real + imag * imag)
         factor = jnp.maximum(modulus - levels, 0.0) / jnp.maximum(modulus, levels)
-        shrunk = jnp.concatenate([real * factor, imag * factor], 0)
-        sparse_new[r] = precise_dot(inv_ref[...], shrunk, ((1,), (0,)))
-        stores.append(
-            pltpu.make_async_copy(sparse_new.at[r], sparse_out.at[r], store_sem.at[2 * r + 1])
-        )
-        stores[-1].start()
+        shrunk_high, shrunk_low = halves(jnp.concatenate([real * factor, imag * factor], 0))
+        sparse = narrow_dot(inv_high[...], shrunk_high, INNER) + (
+            narrow_dot(inv_low[...], shrunk_high, INNER) + narrow_dot(inv_high[...], shrunk_low, INNER)
+        )
+        for i in range(together):
+            r = first + i
+            low_new[r] = both[:columns, i * cols : (i + 1) * cols]
+            sparse_new[r] = sparse[:, i * cols : (i + 1) * cols]
+            stores += [
+                pltpu.make_async_copy(low_new.at[r], low_out.at[r], store_sem.at[2 * r]),
+                pltpu.make_async_copy(sparse_new.at[r], sparse_out.at[r], store_sem.at[2 * r + 1]),
+            ]
+            stores[-2].start()
+            stores[-1].start()
     for copy in stores:
         copy.wait()
 
@@ -589,20 +644,30 @@
     low_flat = low_part.reshape(flat)
     sparse_flat = sparse_part.reshape(flat)
     forward, inverse = time_tables(frames)
+    inverse_high = inverse.astype(jnp.bfloat16)
+    inverse_low = (inverse - inverse_high.astype(np.float32)).astype(jnp.bfloat16)
     dma = pltpu.SemaphoreType.DMA
     bf16, f32 = jnp.bfloat16, jnp.float32
     exchanged = (steps, n_cuts) if direct else (1, 1)
-    smem = pl.BlockSpec(memory_space=pltpu.SMEM)
-    hbm = HBM
-    pieces, basis = pl.pallas_call(
+    flat_wide = (columns, rows_here * cols)
+    high, low, turned, basis = pl.pallas_call(
         functools.partial(fused_kernel, n_cuts, n_coil, inner_cuts, group, direct),
         out_shape=(
-            jax.ShapeDtypeStruct((n_coil, steps, rows_here, 2, group, cols), f32),
+            jax.ShapeDtypeStruct(flat_wide, bf16),
+            jax.ShapeDtypeStruct(flat_wide, bf16),
+            jax.ShapeDtypeStruct(flat_wide, f32),
             jax.ShapeDtypeStruct((rank, columns), f32),
         ),
-        in_specs=[smem] + [hbm] * 12,
-        out_specs=(VMEM, VMEM),
+        in_specs=[HBM] * 14,
+        out_specs=(HBM, HBM, HBM, VMEM),
         scratch_shapes=[
+            pltpu.VMEM((n_coil, steps, rows_here, 2, group, cols), f32),
+            pltpu.VMEM((columns, columns), f32),
+            pltpu.VMEM(flat_wide, bf16),
+            pltpu.VMEM(flat_wide, bf16),
+            pltpu.VMEM(flat_wide, f32),
+            pltpu.VMEM(flat_wide, f32),
+            pltpu.SMEM(band_start.shape[::-1], jnp.int32),
             pltpu.VMEM(wide.shape, bf16),
             pltpu.VMEM(rowtab.shape, f32),
             pltpu.VMEM(coltab.shape, bf16),
@@ -617,6 +682,7 @@
             pltpu.VMEM((here, blocks, taps, block_len), bf16),
             pltpu.VMEM(flat, f32),
             pltpu.VMEM(flat, f32),
+            pltpu.VMEM((group * blocks, 2 * coils, block_len), f32),
             pltpu.VMEM((here, KX, blocks * block_len), bf16),
             pltpu.VMEM((here, 2 * rows, blocks * block_len), f32),
             pltpu.VMEM((blocks * BAND, blocks * block_len), bf16),
@@ -643,7 +709,8 @@
             dma((outer,)),
             dma((plane,)),
             dma((plane,)),
-            dma((10,)),
+            dma((12,)),
+            dma((3,)),
             dma((2 * steps + 1,)),
         ],
         compiler_params=pltpu.CompilerParams(
@@ -653,6 +720,7 @@
     )(
         band_start.T, wide, rowtab, coltab, basis_old.T, data, maps,
         row_offset, col_offset, weight_rows, weight_cols, low_flat, sparse_flat,
+        jnp.asarray(forward),
     )
     low_new, sparse_new, basis = pl.pallas_call(
         finish_kernel,
@@ -661,25 +729,26 @@
             jax.ShapeDtypeStruct(flat, f32),
             jax.ShapeDtypeStruct((rank, columns), f32),
         ),
-        in_specs=[HBM] * 7,
+        in_specs=[HBM] * 8,
         out_specs=(HBM, HBM, HBM),
         scratch_shapes=[
-            pltpu.VMEM(pieces.shape, f32),
+            pltpu.VMEM((rank, columns), f32),
+            pltpu.VMEM((1, frames), f32),
+            pltpu.VMEM(flat_wide, bf16),
+            pltpu.VMEM(flat_wide, bf16),
+            pltpu.VMEM(flat_wide, f32),
+            pltpu.VMEM((columns, columns), f32),
+            pltpu.VMEM((columns, columns), bf16),
+            pltpu.VMEM((columns, columns), bf16),
             pltpu.VMEM(flat, f32),
             pltpu.VMEM(flat, f32),
-            pltpu.VMEM((rank, columns), f32),
-            pltpu.VMEM((1, frames), f32),
-            pltpu.VMEM((columns, columns), f32),
-            pltpu.VMEM((columns, columns), f32),
-            pltpu.VMEM(flat, f32),
-            pltpu.VMEM(flat, f32),
-            dma((7,)),
+            dma((8,)),
             dma((2 * rows_here + 1,)),
         ],
         name="finish",
     )(
-        pieces, low_flat, sparse_flat, basis, thresholds.reshape(1, frames),
-        jnp.asarray(forward), jnp.asarray(inverse),
+        basis, thresholds.reshape(1, frames), high, low, turned, jnp.asarray(forward),
+        jnp.asarray(inverse_high), jnp.asarray(inverse_low),
     )
     return low_new.reshape(low_part.shape), sparse_new.reshape(low_part.shape), basis.T
 

time: 59.9 us -> 53.9 us (0.90)
  Pallas kernels: 58.9 us -> 53 us
    pallas_call x1, Pallas kernels: 54.1 us -> 49.2 us  [local(): pl.pallas_call(functools.partial(fused_kernel, n_cuts, n_coil, inner_cuts...]
    pallas_call x1, Pallas kernels: 4.8 us -> 3.85 us  [local(): pl.pallas_call(finish_kernel, out_shape=(jax.ShapeDtypeStruct(flat, f32),...]
where the time goes in v2:
time: 53.9 us; the launch traced here: 53.7 us
  Pallas kernels  53 us (98%)
  between operations  0.64 us (1%)
    pallas_call x1, Pallas kernels, local(): pl.pallas_call(functools.partial(fused_kernel, n_cuts, n_coil, inner_cuts...  49.2 us
    pallas_call x1, Pallas kernels, local(): pl.pallas_call(finish_kernel, out_shape=(jax.ShapeDtypeStruct(flat, f32),...  3.85 us

profile of v2, /device:TPU:0, one launch (start us, length us, event | category | flops | bytes accessed | tf_op | source)
XLA Modules:
  0.0 53.7 jit_solution(4394357286927394706)
XLA Ops:
  0.6 49.2 %back_and_basis.1 = (bf16[96,1024]{1,0:T(8,128)(2,1)}, bf16[96,1024]{1,0:T(8,128)(2,1)}, f32[96,1024]{1,0:T(8,128)}, f32[32,96]{1,0:T(8,128)}) custom-call(s32[8,48]{1,0:T(8,128)} %bitcast.11, bf16[128,128]{1,0:T(8,128)(2,1)} %constant.12.clone.tab_hbm, f32[256,32]{1,0:T(8,128)} %constant.13.clone.rowtab_hbm, bf16[512,256]{1,0:T(8,128)(2,1)} %constant.14.clone.coltab_hbm, ...), custom_call_target="tpu_custom_call" | custom-call | tf_op jit(solution)/shard_map/back_and_basis/pallas_call | solution.py:653
  49.8 3.8 %finish.1 = (f32[8,96,128]{2,1,0:T(8,128)}, f32[8,96,128]{2,1,0:T(8,128)}, f32[32,96]{1,0:T(8,128)}) custom-call(f32[32,96]{1,0:T(8,128)} %get-tuple-element.10.basis_hbm, f32[1,48]{1,0:T(1,128)} %bitcast.12, bf16[96,1024]{1,0:T(8,128)(2,1)} %get-tuple-element.11.high_hbm, bf16[96,1024]{1,0:T(8,128)(2,1)} %get-tuple-element.12.low_hbm, ...), custom_call_target="tpu_custom_call" | custom-call | tf_op jit(solution)/shard_map/finish/pallas_call | solution.py:725

commit v3 on v2

--- a/solution.py
+++ b/solution.py
@@ -14,10 +14,12 @@
 KX = 256
 BAND = 16
 LANES = 128
-PAIR = 2
+PAIR = 4
+AHEAD = 2
 
 PRECISE = lax.Precision.HIGHEST
 MESH = pl.DeviceIdType.MESH
+LOGICAL = pl.DeviceIdType.LOGICAL
 VMEM = pl.BlockSpec(memory_space=pltpu.VMEM)
 HBM = pl.BlockSpec(memory_space=pltpu.HBM)
 
@@ -127,10 +129,10 @@
         for i in range(batch):
             j = first + i
             inverse = 1.0 / wide[i][j : j + 1]
-            factor = jnp.where(row_ids > j, wide[i] * inverse, 0.0)
+            column = jnp.where(row_ids > j, wide[i], 0.0)
             for k in range(i + 1, batch):
-                wide[k] = wide[k] - factor * wide[k][j : j + 1]
-            joint = joint - factor * joint[j : j + 1]
+                wide[k] = wide[k] - column * wide[k][j : j + 1] * inverse
+            joint = joint - column * joint[j : j + 1] * inverse
             scale = jnp.where(row_ids == j, inverse, scale)
     return joint[:, :columns] * jnp.sqrt(scale[:, :columns])
 
@@ -167,15 +169,16 @@
     barrier = pltpu.get_barrier_semaphore()
     stride = next(k for k in range(3 * n // 8, n + 2) if math.gcd(k, n) == 1)
 
+    def everything(like, send_sem, recv_sem):
+        return [pltpu.make_async_copy(like, like, sem) for sem in (send_sem, recv_sem)]
+
     def place(d):
-        target = lax.rem(flat + d * stride, n)
-        return target // n_coil, lax.rem(target, n_coil)
-
-    def greet(d, carry):
-        pl.semaphore_signal(barrier, inc=1, device_id=place(d), device_id_type=MESH)
-        return carry
-
-    lax.fori_loop(1, n, greet, 0)
+        return lax.rem(flat + d * stride, n)
+
+    def greet(target):
+        pl.semaphore_signal(barrier, inc=1, device_id=target, device_id_type=LOGICAL)
+
+    run(place, 1, n, greet, 8)
 
     mine = pl.ds(me_h * here, here)
     local_copies = [
@@ -206,19 +209,22 @@
 
     def own_first(g):
         return pltpu.make_async_copy(
-            own_part(g, me_c, me_h), rbuf.at[g, me_c, me_h], own_sem.at[g]
+            own_part(g, me_c, me_h), rbuf.at[g, flat], own_sem.at[g]
         )
 
     def first(g, d):
-        t_c, t_h = place(d)
+        target = place(d)
         return pltpu.make_async_remote_copy(
-            src_ref=own_part(g, t_c, t_h),
-            dst_ref=rbuf.at[g, me_c, me_h],
-            send_sem=send1.at[g * n + d],
-            recv_sem=recv1.at[g * n + d],
-            device_id=(t_c, t_h),
-            device_id_type=MESH,
-        )
+            src_ref=own_part(g, target // n_coil, lax.rem(target, n_coil)),
+            dst_ref=rbuf.at[g, flat],
+            send_sem=send1.at[g],
+            recv_sem=recv1.at[g],
+            device_id=target,
+            device_id_type=LOGICAL,
+        )
+
+    def all_first(g):
+        return everything(rbuf.at[g, pl.ds(0, n - 1)], send1.at[g], recv1.at[g])
 
     def own_second(g):
         return pltpu.make_async_copy(
@@ -230,11 +236,15 @@
         return pltpu.make_async_remote_copy(
             src_ref=sbuf.at[g, t_c],
             dst_ref=samples.at[g, :, own_at],
-            send_sem=send2.at[g * n_cuts + d],
-            recv_sem=recv2.at[g * n_cuts + d],
-            device_id=(t_c, me_h),
-            device_id_type=MESH,
-        )
+            send_sem=send2.at[g],
+            recv_sem=recv2.at[g],
+            device_id=t_c * n_coil + me_h,
+            device_id_type=LOGICAL,
+        )
+
+    def all_second(g):
+        span = pl.ds(0, (n_cuts - 1) * chunk)
+        return everything(samples.at[g, :, span], send2.at[g], recv2.at[g])
 
     def maps_copy(d):
         return pltpu.make_async_remote_copy(
@@ -252,8 +262,8 @@
         return pltpu.make_async_remote_copy(
             src_ref=back.at[g, pl.ds(t_h * rows_here, rows_here)],
             dst_ref=pieces.at[me_h, g],
-            send_sem=send4.at[i],
-            recv_sem=recv4.at[i],
+            send_sem=send4.at[0],
+            recv_sem=recv4.at[0],
             device_id=(me_c, t_h),
             device_id_type=MESH,
         )
@@ -282,7 +292,8 @@
 
     def mix(g):
         own_first(g).wait()
-        run(functools.partial(first, g), 1, n, wait)
+        for copy in all_first(g):
+            copy.wait()
         if g == 0:
             tab_copy.wait()
         gathered = rbuf[g].reshape(tab_ref.shape[1], chunk)
@@ -300,7 +311,7 @@
     ids = lax.broadcasted_iota(jnp.int32, (1, tile, block_len), 1).astype(jnp.float32).astype(packed)
     none = jnp.zeros_like(ids)
 
-    def weights(f, carry):
+    def weights(f, slot):
         offsets = coff_ref[f]
         places = (offsets // tile).astype(jnp.float32)
         inside = (offsets % tile).astype(jnp.float32)
@@ -309,11 +320,11 @@
             lanes = slice(b * block_len, (b + 1) * block_len)
             band = slice(b * BAND, (b + 1) * BAND)
             taps = wrow_ref[f, b]
-            band_w[band, lanes] = tap_weights(
+            band_w[slot, band, lanes] = tap_weights(
                 ids - spread(row_at[b : b + 1]), [spread(taps[t : t + 1]) for t in range(taps.shape[0])]
             ).astype(packed).reshape(BAND, block_len)
             first_row = start_ref[b, me_h * here + f]
-            rtab[band, :] = rowtab_ref[pl.ds(first_row, BAND), :].astype(packed)
+            rtab[slot, band, :] = rowtab_ref[pl.ds(first_row, BAND), :].astype(packed)
             taps = wcol_ref[f, b]
             taps = [spread(taps[t : t + 1]) for t in range(taps.shape[0])]
             distance = ids - spread(inside[b : b + 1])
@@ -323,24 +334,32 @@
                 spill = jnp.where(distance == t - tile, taps[t], spill)
             place = spread(places[b : b + 1])
             before = None
+            built = []
             for i in range(KX // tile):
                 hit = place == i
                 value = jnp.where(hit, first, none if before is None else jnp.where(before, spill, none))
-                col_all[f, i * tile : (i + 1) * tile, lanes] = value.reshape(tile, block_len)
+                built.append(value.reshape(tile, block_len))
                 before = hit
+            col_all[f, lanes, :] = jnp.transpose(jnp.concatenate(built, 0))
         factors[f] = lax.dot_general(
-            rtab[...], band_w[...], (((0,), (0,)), ((), ())), preferred_element_type=jnp.float32
-        )
-        return carry
+            rtab[slot], band_w[slot], (((0,), (0,)), ((), ())),
+            preferred_element_type=jnp.float32,
+        )
 
     def ahead(low, high):
-        lax.fori_loop(low, high, weights, 0)
+        def several(i, carry):
+            for j in range(AHEAD):
+                weights(low + i * AHEAD + j, j)
+            return carry
+
+        lax.fori_loop(0, (high - low) // AHEAD, several, 0)
 
     band_w[...] = jnp.zeros_like(band_w)
     if direct:
         marks = [here // 6]
         for i in range(steps):
             marks.append(here - (here - marks[0]) * 2 * (steps - 1 - i) // (5 * max(1, steps - 1)))
+        marks = [mark // AHEAD * AHEAD for mark in marks]
         ahead(0, marks[0])
         pl.semaphore_wait(barrier, n - 1)
         for g in range(steps):
@@ -359,7 +378,8 @@
     def images_of(g, carry):
         if direct:
             own_second(g).wait()
-            run(functools.partial(second, g), 1, n_cuts, wait)
+            for copy in all_second(g):
+                copy.wait()
 
         for i in range(group * blocks):
             wave[i] = samples[g, :, i * block_len : (i + 1) * block_len].astype(jnp.float32)
@@ -378,7 +398,7 @@
                     turned += [real * cosine - imag * sine, real * sine + imag * cosine]
                 parts.append(jnp.concatenate(turned, 0).astype(packed))
             spec = lax.dot_general(
-                jnp.concatenate(parts, 1), col_all[at_frame], (((1,), (1,)), ((), ())),
+                jnp.concatenate(parts, 1), col_all[at_frame], (INNER, ((), ())),
                 preferred_element_type=jnp.float32,
             ).astype(packed)
             for c in range(coils):
@@ -388,12 +408,14 @@
                         q * KX : (q + 1) * KX,
                     ] = spec[(2 * c + q) * rows : (2 * c + q + 1) * rows]
 
+        pair = math.gcd(group, PAIR)
+
         def several(i, inner_carry):
-            for j in range(PAIR):
-                frame(i * PAIR + j)
+            for j in range(pair):
+                frame(i * pair + j)
             return inner_carry
 
-        lax.fori_loop(0, group // PAIR, several, 0)
+        lax.fori_loop(0, group // pair, several, 0)
         images = jnp.dot(spectra[...], coltab_ref[...], preferred_element_type=jnp.float32)
         for f in range(group):
             real = 0.0
@@ -414,7 +436,8 @@
     lax.fori_loop(0, steps, images_of, 0)
     for g in range(steps):
         pieces[me_h, g] = back[g, pl.ds(me_h * rows_here, rows_here)]
-    run(back_copy, 0, steps * (n_coil - 1), wait)
+    for copy in everything(pieces.at[pl.ds(0, n_coil - 1)], send4.at[0], recv4.at[0]):
+        copy.wait()
 
     for r in range(rows_here):
         lanes = slice(r * cols, (r + 1) * cols)
@@ -449,8 +472,8 @@
         return pltpu.make_async_remote_copy(
             src_ref=gram_own.at[target],
             dst_ref=gram_in.at[me_plane],
-            send_sem=send5.at[d],
-            recv_sem=recv5.at[d],
+            send_sem=send5.at[0],
+            recv_sem=recv5.at[0],
             device_id=device,
             device_id_type=MESH,
         )
@@ -460,8 +483,8 @@
         return pltpu.make_async_remote_copy(
             src_ref=part_own,
             dst_ref=part_in.at[me_outer],
-            send_sem=send6.at[d],
-            recv_sem=recv6.at[d],
+            send_sem=send6.at[0],
+            recv_sem=recv6.at[0],
             device_id=(target * inner_cuts + lax.rem(me_c, inner_cuts), me_h),
             device_id_type=MESH,
         )
@@ -471,8 +494,8 @@
         return pltpu.make_async_remote_copy(
             src_ref=sum_own,
             dst_ref=gram_all.at[me_plane],
-            send_sem=send7.at[d],
-            recv_sem=recv7.at[d],
+            send_sem=send7.at[0],
+            recv_sem=recv7.at[0],
             device_id=device,
             device_id_type=MESH,
         )
@@ -490,21 +513,24 @@
     ]
     for copy in outputs:
         copy.start()
-    run(scatter, 1, plane, wait)
+    for copy in everything(gram_in.at[pl.ds(0, plane - 1)], send5.at[0], recv5.at[0]):
+        copy.wait()
     value = gram_in[0]
     for i in range(1, plane):
         value = value + gram_in[i]
     part_own[...] = value
     run(across, 1, outer_cuts, start)
     part_in[me_outer] = value
-    run(across, 1, outer_cuts, wait)
+    for copy in everything(part_in.at[pl.ds(0, outer_cuts - 1)], send6.at[0], recv6.at[0]):
+        copy.wait()
     value = part_in[0]
     for i in range(1, outer_cuts):
         value = value + part_in[i]
     sum_own[...] = value
     run(gather, 1, plane, start)
     gram_all[me_plane] = value
-    run(gather, 1, plane, wait)
+    for copy in everything(gram_all.at[pl.ds(0, plane - 1)], send7.at[0], recv7.at[0]):
+        copy.wait()
     gram = jnp.concatenate([gram_all[i] for i in range(plane)], 0)
 
     basis = basis_ref[...]
@@ -672,7 +698,7 @@
             pltpu.VMEM(rowtab.shape, f32),
             pltpu.VMEM(coltab.shape, bf16),
             pltpu.VMEM((rank, columns), f32),
-            pltpu.VMEM(exchanged + (n_coil, radial.shape[0], 2, chunk), bf16),
+            pltpu.VMEM((exchanged[0], n, radial.shape[0], 2, chunk), bf16),
             pltpu.VMEM(exchanged + (2 * coils, chunk), bf16),
             pltpu.VMEM((steps, 2 * coils, group_len), bf16),
             pltpu.VMEM((coils,) + coil_maps.shape[1:], bf16),
@@ -683,10 +709,10 @@
             pltpu.VMEM(flat, f32),
             pltpu.VMEM(flat, f32),
             pltpu.VMEM((group * blocks, 2 * coils, block_len), f32),
-            pltpu.VMEM((here, KX, blocks * block_len), bf16),
+            pltpu.VMEM((here, blocks * block_len, KX), bf16),
             pltpu.VMEM((here, 2 * rows, blocks * block_len), f32),
-            pltpu.VMEM((blocks * BAND, blocks * block_len), bf16),
-            pltpu.VMEM((blocks * BAND, 2 * rows), bf16),
+            pltpu.VMEM((AHEAD, blocks * BAND, blocks * block_len), bf16),
+            pltpu.VMEM((AHEAD, blocks * BAND, 2 * rows), bf16),
             pltpu.VMEM((group * coils * rows, 2 * KX), bf16),
             pltpu.VMEM((steps, rows, 2, group, cols), f32),
             pltpu.VMEM((plane, piece, columns), f32),
@@ -695,20 +721,20 @@
             pltpu.VMEM((outer, piece, columns), f32),
             pltpu.VMEM((piece, columns), f32),
             pltpu.VMEM((plane, piece, columns), f32),
-            dma((steps * n,)),
-            dma((steps * n,)),
-            dma((steps * n_cuts,)),
-            dma((steps * n_cuts,)),
+            dma((steps,)),
+            dma((steps,)),
+            dma((steps,)),
+            dma((steps,)),
             dma((n_coil,)),
             dma((n_coil,)),
-            dma((steps * n_coil,)),
-            dma((steps * n_coil,)),
-            dma((plane,)),
-            dma((plane,)),
-            dma((outer,)),
-            dma((outer,)),
-            dma((plane,)),
-            dma((plane,)),
+            dma((1,)),
+            dma((1,)),
+            dma((1,)),
+            dma((1,)),
+            dma((1,)),
+            dma((1,)),
+            dma((1,)),
+            dma((1,)),
             dma((12,)),
             dma((3,)),
             dma((2 * steps + 1,)),

time: 53.9 us -> 49.5 us (0.918)
  Pallas kernels: 53 us -> 48.6 us
    pallas_call x1, Pallas kernels: 49.2 us -> 44.8 us  [local(): pl.pallas_call(functools.partial(fused_kernel, n_cuts, n_coil, inner_cuts...]
where the time goes in v3:
time: 49.5 us; the launch traced here: 49.3 us
  Pallas kernels  48.6 us (98%)
  between operations  0.64 us (1%)
    pallas_call x1, Pallas kernels, local(): pl.pallas_call(functools.partial(fused_kernel, n_cuts, n_coil, inner_cuts...  44.8 us
    pallas_call x1, Pallas kernels, local(): pl.pallas_call(finish_kernel, out_shape=(jax.ShapeDtypeStruct(flat, f32),...  3.85 us

profile of v3, /device:TPU:0, one launch (start us, length us, event | category | flops | bytes accessed | tf_op | source)
XLA Modules:
  0.0 49.3 jit_solution(16234048029352749430)
XLA Ops:
  0.6 44.8 %back_and_basis.1 = (bf16[96,1024]{1,0:T(8,128)(2,1)}, bf16[96,1024]{1,0:T(8,128)(2,1)}, f32[96,1024]{1,0:T(8,128)}, f32[32,96]{1,0:T(8,128)}) custom-call(s32[8,48]{1,0:T(8,128)} %bitcast.11, bf16[128,128]{1,0:T(8,128)(2,1)} %constant.12.clone.tab_hbm, f32[256,32]{1,0:T(8,128)} %constant.13.clone.rowtab_hbm, bf16[512,256]{1,0:T(8,128)(2,1)} %constant.14.clone.coltab_hbm, ...), custom_call_target="tpu_custom_call" | custom-call | tf_op jit(solution)/shard_map/back_and_basis/pallas_call | solution.py:679
  45.4 3.8 %finish.1 = (f32[8,96,128]{2,1,0:T(8,128)}, f32[8,96,128]{2,1,0:T(8,128)}, f32[32,96]{1,0:T(8,128)}) custom-call(f32[32,96]{1,0:T(8,128)} %get-tuple-element.10.basis_hbm, f32[1,48]{1,0:T(1,128)} %bitcast.12, bf16[96,1024]{1,0:T(8,128)(2,1)} %get-tuple-element.11.high_hbm, bf16[96,1024]{1,0:T(8,128)(2,1)} %get-tuple-element.12.low_hbm, ...), custom_call_target="tpu_custom_call" | custom-call | tf_op jit(solution)/shard_map/finish/pallas_call | solution.py:751

commit v4 on v3

--- a/solution.py
+++ b/solution.py
@@ -16,6 +16,7 @@
 LANES = 128
 PAIR = 4
 AHEAD = 2
+LATER = 0
 
 PRECISE = lax.Precision.HIGHEST
 MESH = pl.DeviceIdType.MESH
@@ -73,8 +74,11 @@
             action(make(low + i * width + j))
         return carry
 
-    count = (high - low) // width if width > 1 else high - low
-    lax.fori_loop(0, count, step, 0)
+    count = (high - low) // width
+    if width > 1 and count == 1:
+        step(0, 0)
+    else:
+        lax.fori_loop(0, count, step, 0)
     if width > 1:
         for d in range(low + count * width, high):
             action(make(d))
@@ -144,7 +148,7 @@
     high_out, low_out, turned_out, basis_out,
     pieces, fwd_ref, high, low, whole, turned,
     start_ref, tab_ref, rowtab_ref, coltab_ref, basis_ref, rbuf, sbuf, samples, maps_all, roff_ref, coff_ref, wrow_ref, wcol_ref, low_ref, sparse_ref,
-    wave, col_all, factors, band_w, rtab, spectra, back, gram_own, gram_in, part_own, part_in, sum_own, gram_all,
+    wave, col_all, factors, band_w, rtab, spectra, back, sent, gram_own, gram_in, part_own, part_in, sum_own, gram_all,
     send1, recv1, send2, recv2, send3, recv3, send4, recv4, send5, recv5, send6, recv6,
     send7, recv7, local_sem, out_sem, own_sem,
 ):
@@ -260,7 +264,7 @@
         g = i // (n_coil - 1)
         t_h = lax.rem(me_h + 1 + lax.rem(i, n_coil - 1), n_coil)
         return pltpu.make_async_remote_copy(
-            src_ref=back.at[g, pl.ds(t_h * rows_here, rows_here)],
+            src_ref=sent.at[g, pl.ds(t_h * rows_here, rows_here)],
             dst_ref=pieces.at[me_h, g],
             send_sem=send4.at[0],
             recv_sem=recv4.at[0],
@@ -287,9 +291,6 @@
     late_copies = local_copies[6:] + ([] if direct else [tab_copy])
     for copy in local_copies[6:]:
         copy.start()
-    for copy in local_copies[:6]:
-        copy.wait()
-
     def mix(g):
         own_first(g).wait()
         for copy in all_first(g):
@@ -356,20 +357,23 @@
 
     band_w[...] = jnp.zeros_like(band_w)
     if direct:
-        marks = [here // 6]
-        for i in range(steps):
-            marks.append(here - (here - marks[0]) * 2 * (steps - 1 - i) // (5 * max(1, steps - 1)))
-        marks = [mark // AHEAD * AHEAD for mark in marks]
-        ahead(0, marks[0])
+        marks = [0] + [
+            (here - here * LATER * (steps - 1 - i) // (12 * max(1, steps - 1))) // AHEAD * AHEAD
+            for i in range(steps)
+        ]
         pl.semaphore_wait(barrier, n - 1)
         for g in range(steps):
             run(functools.partial(first, g), 1, n, start, 4)
         run(maps_copy, 1, n_coil, start)
+        for copy in local_copies[:6]:
+            copy.wait()
         for g in range(steps):
             ahead(marks[g], marks[g + 1])
             mix(g)
         run(maps_copy, 1, n_coil, wait)
     else:
+        for copy in local_copies[:6]:
+            copy.wait()
         ahead(0, here)
     own_maps.wait()
     for copy in late_copies:
@@ -430,12 +434,13 @@
                 imag = imag + (image_im * sens_re - image_re * sens_im)
             back[g, :, 0, f, :] = real
             back[g, :, 1, f, :] = imag
+        sent[g] = back[g].astype(packed)
         run(back_copy, g * (n_coil - 1), (g + 1) * (n_coil - 1), start)
         return carry
 
     lax.fori_loop(0, steps, images_of, 0)
     for g in range(steps):
-        pieces[me_h, g] = back[g, pl.ds(me_h * rows_here, rows_here)]
+        pieces[me_h, g] = sent[g, pl.ds(me_h * rows_here, rows_here)]
     for copy in everything(pieces.at[pl.ds(0, n_coil - 1)], send4.at[0], recv4.at[0]):
         copy.wait()
 
@@ -443,7 +448,7 @@
         lanes = slice(r * cols, (r + 1) * cols)
         part = jnp.concatenate(
             [
-                pieces[h, g, r, p]
+                pieces[h, g, r, p].astype(jnp.float32)
                 for p in range(2)
                 for h in range(n_coil)
                 for g in range(steps)
@@ -463,46 +468,37 @@
     me_outer = me_c // inner_cuts
     piece = columns // plane
 
-    def plane_place(d):
-        target = lax.rem(me_plane + d, plane)
-        return target, (me_outer * inner_cuts + target // n_coil, lax.rem(target, n_coil))
+    def in_plane(source, target, sems, d):
+        peer = lax.rem(me_plane + d, plane)
+        return pltpu.make_async_remote_copy(
+            src_ref=source(peer),
+            dst_ref=target.at[me_plane],
+            send_sem=sems[0].at[0],
+            recv_sem=sems[1].at[0],
+            device_id=me_outer * plane + peer,
+            device_id_type=LOGICAL,
+        )
 
     def scatter(d):
-        target, device = plane_place(d)
-        return pltpu.make_async_remote_copy(
-            src_ref=gram_own.at[target],
-            dst_ref=gram_in.at[me_plane],
-            send_sem=send5.at[0],
-            recv_sem=recv5.at[0],
-            device_id=device,
-            device_id_type=MESH,
-        )
+        return in_plane(lambda peer: gram_own.at[peer], gram_in, (send5, recv5), d)
 
     def across(d):
-        target = lax.rem(me_outer + d, outer_cuts)
+        peer = lax.rem(me_outer + d, outer_cuts)
         return pltpu.make_async_remote_copy(
             src_ref=part_own,
             dst_ref=part_in.at[me_outer],
             send_sem=send6.at[0],
             recv_sem=recv6.at[0],
-            device_id=(target * inner_cuts + lax.rem(me_c, inner_cuts), me_h),
-            device_id_type=MESH,
+            device_id=peer * plane + me_plane,
+            device_id_type=LOGICAL,
         )
 
     def gather(d):
-        target, device = plane_place(d)
-        return pltpu.make_async_remote_copy(
-            src_ref=sum_own,
-            dst_ref=gram_all.at[me_plane],
-            send_sem=send7.at[0],
-            recv_sem=recv7.at[0],
-            device_id=device,
-            device_id_type=MESH,
-        )
+        return in_plane(lambda peer: sum_own, gram_all, (send7, recv7), d)
 
     for i in range(plane):
         gram_own[i] = gram[i * piece : (i + 1) * piece]
-    run(scatter, 1, plane, start)
+    run(scatter, 1, plane, start, 7)
     gram_in[me_plane] = gram_own[me_plane]
     turned[...] = precise_dot(fwd_ref[...], whole[...], ((1,), (0,)))
     outputs = [
@@ -519,7 +515,7 @@
     for i in range(1, plane):
         value = value + gram_in[i]
     part_own[...] = value
-    run(across, 1, outer_cuts, start)
+    run(across, 1, outer_cuts, start, 3)
     part_in[me_outer] = value
     for copy in everything(part_in.at[pl.ds(0, outer_cuts - 1)], send6.at[0], recv6.at[0]):
         copy.wait()
@@ -527,7 +523,7 @@
     for i in range(1, outer_cuts):
         value = value + part_in[i]
     sum_own[...] = value
-    run(gather, 1, plane, start)
+    run(gather, 1, plane, start, 7)
     gram_all[me_plane] = value
     for copy in everything(gram_all.at[pl.ds(0, plane - 1)], send7.at[0], recv7.at[0]):
         copy.wait()
@@ -568,7 +564,7 @@
         copy.start()
     for copy in loads[:3]:
         copy.wait()
-    stores = [pltpu.make_async_copy(basis_ref, basis_out, store_sem.at[2 * rows_here])]
+    stores = [pltpu.make_async_copy(basis_ref, basis_out, store_sem.at[0])]
     stores[0].start()
     basis = basis_ref[...]
     project = precise_dot(basis, basis, ((0,), (0,)))
@@ -581,6 +577,14 @@
     for copy in loads[3:]:
         copy.wait()
     together = math.gcd(rows_here, 2)
+
+    def send(source, target, first):
+        rows = pl.ds(first, together)
+        stores.append(
+            pltpu.make_async_copy(source.at[rows], target.at[rows], store_sem.at[len(stores)])
+        )
+        stores[-1].start()
+
     for first in range(0, rows_here, together):
         lanes = slice(first * cols, (first + together) * cols)
         high = high_ref[:, lanes]
@@ -592,19 +596,15 @@
         modulus = jnp.sqrt(real * real + imag * imag)
         factor = jnp.maximum(modulus - levels, 0.0) / jnp.maximum(modulus, levels)
         shrunk_high, shrunk_low = halves(jnp.concatenate([real * factor, imag * factor], 0))
+        for i in range(together):
+            low_new[first + i] = both[:columns, i * cols : (i + 1) * cols]
+        send(low_new, low_out, first)
         sparse = narrow_dot(inv_high[...], shrunk_high, INNER) + (
             narrow_dot(inv_low[...], shrunk_high, INNER) + narrow_dot(inv_high[...], shrunk_low, INNER)
         )
         for i in range(together):
-            r = first + i
-            low_new[r] = both[:columns, i * cols : (i + 1) * cols]
-            sparse_new[r] = sparse[:, i * cols : (i + 1) * cols]
-            stores += [
-                pltpu.make_async_copy(low_new.at[r], low_out.at[r], store_sem.at[2 * r]),
-                pltpu.make_async_copy(sparse_new.at[r], sparse_out.at[r], store_sem.at[2 * r + 1]),
-            ]
-            stores[-2].start()
-            stores[-1].start()
+            sparse_new[first + i] = sparse[:, i * cols : (i + 1) * cols]
+        send(sparse_new, sparse_out, first)
     for copy in stores:
         copy.wait()
 
@@ -687,7 +687,7 @@
         in_specs=[HBM] * 14,
         out_specs=(HBM, HBM, HBM, VMEM),
         scratch_shapes=[
-            pltpu.VMEM((n_coil, steps, rows_here, 2, group, cols), f32),
+            pltpu.VMEM((n_coil, steps, rows_here, 2, group, cols), bf16),
             pltpu.VMEM((columns, columns), f32),
             pltpu.VMEM(flat_wide, bf16),
             pltpu.VMEM(flat_wide, bf16),
@@ -715,6 +715,7 @@
             pltpu.VMEM((AHEAD, blocks * BAND, 2 * rows), bf16),
             pltpu.VMEM((group * coils * rows, 2 * KX), bf16),
             pltpu.VMEM((steps, rows, 2, group, cols), f32),
+            pltpu.VMEM((steps, rows, 2, group, cols), bf16),
             pltpu.VMEM((plane, piece, columns), f32),
             pltpu.VMEM((plane, piece, columns), f32),
             pltpu.VMEM((piece, columns), f32),
@@ -769,7 +770,7 @@
             pltpu.VMEM(flat, f32),
             pltpu.VMEM(flat, f32),
             dma((8,)),
-            dma((2 * rows_here + 1,)),
+            dma((1 + 2 * (rows_here // math.gcd(rows_here, 2)),)),
         ],
         name="finish",
     )(

time: 49.5 us -> 48.9 us (0.988)
  Pallas kernels: 48.6 us -> 48 us
    pallas_call x1, Pallas kernels: 44.8 us -> 44.2 us  [local(): pl.pallas_call(functools.partial(fused_kernel, n_cuts, n_coil, inner_cuts...]
where the time goes in v4:
time: 48.9 us; the launch traced here: 48.6 us
  Pallas kernels  48 us (98%)
  between operations  0.64 us (1%)
    pallas_call x1, Pallas kernels, local(): pl.pallas_call(functools.partial(fused_kernel, n_cuts, n_coil, inner_cuts...  44.2 us
    pallas_call x1, Pallas kernels, local(): pl.pallas_call(finish_kernel, out_shape=(jax.ShapeDtypeStruct(flat, f32),...  3.77 us

profile of v4, /device:TPU:0, one launch (start us, length us, event | category | flops | bytes accessed | tf_op | source)
XLA Modules:
  0.0 48.6 jit_solution(3643867198483221064)
XLA Ops:
  0.6 44.2 %back_and_basis.1 = (bf16[96,1024]{1,0:T(8,128)(2,1)}, bf16[96,1024]{1,0:T(8,128)(2,1)}, f32[96,1024]{1,0:T(8,128)}, f32[32,96]{1,0:T(8,128)}) custom-call(s32[8,48]{1,0:T(8,128)} %bitcast.11, bf16[128,128]{1,0:T(8,128)(2,1)} %constant.12.clone.tab_hbm, f32[256,32]{1,0:T(8,128)} %constant.13.clone.rowtab_hbm, bf16[512,256]{1,0:T(8,128)(2,1)} %constant.14.clone.coltab_hbm, ...), custom_call_target="tpu_custom_call" | custom-call | tf_op jit(solution)/shard_map/back_and_basis/pallas_call | solution.py:679
  44.8 3.8 %finish.1 = (f32[8,96,128]{2,1,0:T(8,128)}, f32[8,96,128]{2,1,0:T(8,128)}, f32[32,96]{1,0:T(8,128)}) custom-call(f32[32,96]{1,0:T(8,128)} %get-tuple-element.10.basis_hbm, f32[1,48]{1,0:T(1,128)} %bitcast.12, bf16[96,1024]{1,0:T(8,128)(2,1)} %get-tuple-element.11.high_hbm, bf16[96,1024]{1,0:T(8,128)(2,1)} %get-tuple-element.12.low_hbm, ...), custom_call_target="tpu_custom_call" | custom-call | tf_op jit(solution)/shard_map/finish/pallas_call | solution.py:752

commit v5 on v4

--- a/solution.py
+++ b/solution.py
@@ -118,10 +118,21 @@
     )
 
 
-def orthonormal_rows(powered):
-    rank, columns = powered.shape
-    inner = precise_dot(powered, powered, ((1,), (1,)))
-    joint = jnp.concatenate([powered, inner], 1)
+LEFT = (0, 0, 1, 0, 1, 2)
+RIGHT = (0, 1, 0, 2, 1, 0)
+
+
+def stacked(values, order, axis):
+    high, rest = halves(values)
+    middle, low = halves(values - high.astype(jnp.float32))
+    return jnp.concatenate([(high, middle, low)[i] for i in order], axis)
+
+
+def orthonormal_rows(powered, columns):
+    rank = powered.shape[0]
+    right = stacked(powered, RIGHT, 1)
+    right = jnp.concatenate([jnp.zeros((columns, right.shape[1]), right.dtype), right], 0)
+    joint = powered + narrow_dot(stacked(powered, LEFT, 1), right, LAST)
     row_ids = lax.broadcasted_iota(jnp.int32, joint.shape, 0)
     scale = jnp.ones_like(joint)
     batch = math.gcd(rank, 8)
@@ -138,7 +149,7 @@
                 wide[k] = wide[k] - column * wide[k][j : j + 1] * inverse
             joint = joint - column * joint[j : j + 1] * inverse
             scale = jnp.where(row_ids == j, inverse, scale)
-    return joint[:, :columns] * jnp.sqrt(scale[:, :columns])
+    return joint * jnp.sqrt(scale)
 
 
 def fused_kernel(
@@ -146,7 +157,7 @@
     start_hbm, tab_hbm, rowtab_hbm, coltab_hbm, basis_hbm, radial_ref, maps_ref,
     roff_hbm, coff_hbm, wrow_hbm, wcol_hbm, low_hbm, sparse_hbm, fwd_hbm,
     high_out, low_out, turned_out, basis_out,
-    pieces, fwd_ref, high, low, whole, turned,
+    pieces, full_ref, fwd_ref, high, low, whole, turned,
     start_ref, tab_ref, rowtab_ref, coltab_ref, basis_ref, rbuf, sbuf, samples, maps_all, roff_ref, coff_ref, wrow_ref, wcol_ref, low_ref, sparse_ref,
     wave, col_all, factors, band_w, rtab, spectra, back, sent, gram_own, gram_in, part_own, part_in, sum_own, gram_all,
     send1, recv1, send2, recv2, send3, recv3, send4, recv4, send5, recv5, send6, recv6,
@@ -459,8 +470,11 @@
         merged = low_ref[r] + sparse - part
         whole[:, lanes] = merged
         high[:, lanes], low[:, lanes] = halves(merged - sparse)
-    gram = narrow_dot(high[...], high[...], LAST)
-    gram = gram + narrow_dot(low[...], high[...], LAST) + narrow_dot(high[...], low[...], LAST)
+    upper, lower = high[...], low[...]
+    gram = narrow_dot(
+        jnp.concatenate([upper, lower, upper], 1), jnp.concatenate([upper, upper, lower], 1), LAST
+    )
+    full_ref[...] = jnp.zeros_like(full_ref)
 
     plane = inner_cuts * n_coil
     outer_cuts = n_cuts // inner_cuts
@@ -527,12 +541,16 @@
     gram_all[me_plane] = value
     for copy in everything(gram_all.at[pl.ds(0, plane - 1)], send7.at[0], recv7.at[0]):
         copy.wait()
-    gram = jnp.concatenate([gram_all[i] for i in range(plane)], 0)
-
-    basis = basis_ref[...]
+    for i in range(plane):
+        full_ref[i * piece : (i + 1) * piece, :columns] = gram_all[i]
+    grams = stacked(full_ref[...], RIGHT, 0)
+    rank = basis_ref.shape[0]
+    basis = jnp.concatenate([basis_ref[...], jnp.zeros((rank, rank), jnp.float32)], 1)
     for repeat in range(POWER):
-        basis = orthonormal_rows(precise_dot(basis, gram, ((1,), (0,))))
-    basis_out[...] = basis
+        basis = orthonormal_rows(
+            narrow_dot(stacked(basis, LEFT, 1), grams, INNER), columns
+        )
+    basis_out[...] = basis[:, :columns]
     for copy in outputs:
         copy.wait()
 
@@ -569,17 +587,21 @@
     basis = basis_ref[...]
     project = precise_dot(basis, basis, ((0,), (0,)))
     project = jnp.concatenate([project, precise_dot(fwd_ref[...], project, INNER)], 0)
-    project_high, project_low = halves(project)
+    upper, lower = halves(project)
+    project = jnp.concatenate([upper, lower, upper], 1)
     same = lax.broadcasted_iota(jnp.int32, (frames, frames), 0) == lax.broadcasted_iota(
         jnp.int32, (frames, frames), 1
     )
     levels = jnp.sum(jnp.where(same, level_ref[...], 0.0), axis=1, keepdims=True)
     for copy in loads[3:]:
         copy.wait()
-    together = math.gcd(rows_here, 2)
+    upper, lower = inv_high[...], inv_low[...]
+    inverse = jnp.concatenate([upper, lower, upper], 1)
+    together = math.gcd(rows_here, 4)
+    batch = math.gcd(rows_here, 4)
 
     def send(source, target, first):
-        rows = pl.ds(first, together)
+        rows = pl.ds(first, batch)
         stores.append(
             pltpu.make_async_copy(source.at[rows], target.at[rows], store_sem.at[len(stores)])
         )
@@ -587,24 +609,20 @@
 
     for first in range(0, rows_here, together):
         lanes = slice(first * cols, (first + together) * cols)
-        high = high_ref[:, lanes]
-        both = narrow_dot(project_high, high, INNER) + (
-            narrow_dot(project_low, high, INNER) + narrow_dot(project_high, low_ref[:, lanes], INNER)
-        )
+        upper, lower = high_ref[:, lanes], low_ref[:, lanes]
+        both = narrow_dot(project, jnp.concatenate([upper, upper, lower], 0), INNER)
         spectrum = turned_ref[:, lanes] - both[columns:]
         real, imag = spectrum[:frames], spectrum[frames:]
         modulus = jnp.sqrt(real * real + imag * imag)
         factor = jnp.maximum(modulus - levels, 0.0) / jnp.maximum(modulus, levels)
-        shrunk_high, shrunk_low = halves(jnp.concatenate([real * factor, imag * factor], 0))
+        upper, lower = halves(jnp.concatenate([real * factor, imag * factor], 0))
+        sparse = narrow_dot(inverse, jnp.concatenate([upper, upper, lower], 0), INNER)
         for i in range(together):
             low_new[first + i] = both[:columns, i * cols : (i + 1) * cols]
-        send(low_new, low_out, first)
-        sparse = narrow_dot(inv_high[...], shrunk_high, INNER) + (
-            narrow_dot(inv_low[...], shrunk_high, INNER) + narrow_dot(inv_high[...], shrunk_low, INNER)
-        )
-        for i in range(together):
             sparse_new[first + i] = sparse[:, i * cols : (i + 1) * cols]
-        send(sparse_new, sparse_out, first)
+        if (first + together) % batch == 0:
+            send(low_new, low_out, first + together - batch)
+            send(sparse_new, sparse_out, first + together - batch)
     for copy in stores:
         copy.wait()
 
@@ -688,6 +706,7 @@
         out_specs=(HBM, HBM, HBM, VMEM),
         scratch_shapes=[
             pltpu.VMEM((n_coil, steps, rows_here, 2, group, cols), bf16),
+            pltpu.VMEM((columns + rank, columns + rank), f32),
             pltpu.VMEM((columns, columns), f32),
             pltpu.VMEM(flat_wide, bf16),
             pltpu.VMEM(flat_wide, bf16),
@@ -770,7 +789,7 @@
             pltpu.VMEM(flat, f32),
             pltpu.VMEM(flat, f32),
             dma((8,)),
-            dma((1 + 2 * (rows_here // math.gcd(rows_here, 2)),)),
+            dma((1 + 2 * rows_here // math.gcd(rows_here, 4),)),
         ],
         name="finish",
     )(

time: 48.9 us -> 48 us (0.982)
  Pallas kernels: 48 us -> 47 us
    pallas_call x1, Pallas kernels: 3.77 us -> 3.08 us  [local(): pl.pallas_call(finish_kernel, out_shape=(jax.ShapeDtypeStruct(flat, f32),...]
where the time goes in v5:
time: 48 us; the launch traced here: 47.7 us
  Pallas kernels  47 us (98%)
  between operations  0.64 us (1%)
    pallas_call x1, Pallas kernels, local(): pl.pallas_call(functools.partial(fused_kernel, n_cuts, n_coil, inner_cuts...  44 us
    pallas_call x1, Pallas kernels, local(): pl.pallas_call(finish_kernel, out_shape=(jax.ShapeDtypeStruct(flat, f32),...  3.08 us

profile of v5, /device:TPU:0, one launch (start us, length us, event | category | flops | bytes accessed | tf_op | source)
XLA Modules:
  0.0 47.7 jit_solution(2001843829117226912)
XLA Ops:
  0.6 44.0 %back_and_basis.1 = (bf16[96,1024]{1,0:T(8,128)(2,1)}, bf16[96,1024]{1,0:T(8,128)(2,1)}, f32[96,1024]{1,0:T(8,128)}, f32[32,96]{1,0:T(8,128)}) custom-call(s32[8,48]{1,0:T(8,128)} %bitcast.11, bf16[128,128]{1,0:T(8,128)(2,1)} %constant.12.clone.tab_hbm, f32[256,32]{1,0:T(8,128)} %constant.13.clone.rowtab_hbm, bf16[512,256]{1,0:T(8,128)(2,1)} %constant.14.clone.coltab_hbm, ...), custom_call_target="tpu_custom_call" | custom-call | tf_op jit(solution)/shard_map/back_and_basis/pallas_call | solution.py:697
  44.6 3.1 %finish.1 = (f32[8,96,128]{2,1,0:T(8,128)}, f32[8,96,128]{2,1,0:T(8,128)}, f32[32,96]{1,0:T(8,128)}) custom-call(f32[32,96]{1,0:T(8,128)} %get-tuple-element.10.basis_hbm, f32[1,48]{1,0:T(1,128)} %bitcast.12, bf16[96,1024]{1,0:T(8,128)(2,1)} %get-tuple-element.11.high_hbm, bf16[96,1024]{1,0:T(8,128)(2,1)} %get-tuple-element.12.low_hbm, ...), custom_call_target="tpu_custom_call" | custom-call | tf_op jit(solution)/shard_map/finish/pallas_call | solution.py:771

commit v6 on v5

--- a/solution.py
+++ b/solution.py
@@ -90,6 +90,12 @@
 
 def wait(copy):
     copy.wait()
+
+
+def deep(table):
+    high = table.astype(jnp.bfloat16)
+    low = (table - high.astype(np.float32)).astype(jnp.bfloat16)
+    return np.concatenate([high, low, high], 1)
 
 
 LAST = ((1,), (1,))
@@ -556,9 +562,9 @@
 
 
 def finish_kernel(
-    basis_hbm, level_hbm, high_hbm, low_hbm, turned_hbm, fwd_hbm, inv_high_hbm, inv_low_hbm,
+    basis_hbm, level_hbm, high_hbm, low_hbm, turned_hbm, fwd_hbm, inverse_hbm,
     low_out, sparse_out, basis_out,
-    basis_ref, level_ref, high_ref, low_ref, turned_ref, fwd_ref, inv_high, inv_low,
+    basis_ref, level_ref, high_ref, low_ref, turned_ref, fwd_ref, inverse_ref,
     low_new, sparse_new, load_sem, store_sem,
 ):
     frames = level_ref.shape[1]
@@ -573,8 +579,7 @@
                 (high_hbm, high_ref),
                 (low_hbm, low_ref),
                 (turned_hbm, turned_ref),
-                (inv_high_hbm, inv_high),
-                (inv_low_hbm, inv_low),
+                (inverse_hbm, inverse_ref),
             ]
         )
     ]
@@ -585,9 +590,16 @@
     stores = [pltpu.make_async_copy(basis_ref, basis_out, store_sem.at[0])]
     stores[0].start()
     basis = basis_ref[...]
-    project = precise_dot(basis, basis, ((0,), (0,)))
-    project = jnp.concatenate([project, precise_dot(fwd_ref[...], project, INNER)], 0)
+    upper, lower = halves(basis)
+    project = narrow_dot(
+        jnp.concatenate([upper, lower, upper], 0), jnp.concatenate([upper, upper, lower], 0),
+        ((0,), (0,)),
+    )
     upper, lower = halves(project)
+    turned = narrow_dot(fwd_ref[...], jnp.concatenate([upper, upper, lower], 0), INNER)
+    turned_upper, turned_lower = halves(turned)
+    upper = jnp.concatenate([upper, turned_upper], 0)
+    lower = jnp.concatenate([lower, turned_lower], 0)
     project = jnp.concatenate([upper, lower, upper], 1)
     same = lax.broadcasted_iota(jnp.int32, (frames, frames), 0) == lax.broadcasted_iota(
         jnp.int32, (frames, frames), 1
@@ -595,8 +607,6 @@
     levels = jnp.sum(jnp.where(same, level_ref[...], 0.0), axis=1, keepdims=True)
     for copy in loads[3:]:
         copy.wait()
-    upper, lower = inv_high[...], inv_low[...]
-    inverse = jnp.concatenate([upper, lower, upper], 1)
     together = math.gcd(rows_here, 4)
     batch = math.gcd(rows_here, 4)
 
@@ -616,7 +626,7 @@
         modulus = jnp.sqrt(real * real + imag * imag)
         factor = jnp.maximum(modulus - levels, 0.0) / jnp.maximum(modulus, levels)
         upper, lower = halves(jnp.concatenate([real * factor, imag * factor], 0))
-        sparse = narrow_dot(inverse, jnp.concatenate([upper, upper, lower], 0), INNER)
+        sparse = narrow_dot(inverse_ref[...], jnp.concatenate([upper, upper, lower], 0), INNER)
         for i in range(together):
             low_new[first + i] = both[:columns, i * cols : (i + 1) * cols]
             sparse_new[first + i] = sparse[:, i * cols : (i + 1) * cols]
@@ -688,8 +698,6 @@
     low_flat = low_part.reshape(flat)
     sparse_flat = sparse_part.reshape(flat)
     forward, inverse = time_tables(frames)
-    inverse_high = inverse.astype(jnp.bfloat16)
-    inverse_low = (inverse - inverse_high.astype(np.float32)).astype(jnp.bfloat16)
     dma = pltpu.SemaphoreType.DMA
     bf16, f32 = jnp.bfloat16, jnp.float32
     exchanged = (steps, n_cuts) if direct else (1, 1)
@@ -775,7 +783,7 @@
             jax.ShapeDtypeStruct(flat, f32),
             jax.ShapeDtypeStruct((rank, columns), f32),
         ),
-        in_specs=[HBM] * 8,
+        in_specs=[HBM] * 7,
         out_specs=(HBM, HBM, HBM),
         scratch_shapes=[
             pltpu.VMEM((rank, columns), f32),
@@ -783,18 +791,17 @@
             pltpu.VMEM(flat_wide, bf16),
             pltpu.VMEM(flat_wide, bf16),
             pltpu.VMEM(flat_wide, f32),
-            pltpu.VMEM((columns, columns), f32),
-            pltpu.VMEM((columns, columns), bf16),
-            pltpu.VMEM((columns, columns), bf16),
+            pltpu.VMEM(deep(forward).shape, bf16),
+            pltpu.VMEM(deep(inverse).shape, bf16),
             pltpu.VMEM(flat, f32),
             pltpu.VMEM(flat, f32),
-            dma((8,)),
+            dma((7,)),
             dma((1 + 2 * rows_here // math.gcd(rows_here, 4),)),
         ],
         name="finish",
     )(
-        basis, thresholds.reshape(1, frames), high, low, turned, jnp.asarray(forward),
-        jnp.asarray(inverse_high), jnp.asarray(inverse_low),
+        basis, thresholds.reshape(1, frames), high, low, turned,
+        jnp.asarray(deep(forward)), jnp.asarray(deep(inverse)),
     )
     return low_new.reshape(low_part.shape), sparse_new.reshape(low_part.shape), basis.T
 

time: 48 us -> 47.9 us (level)
  no operation moved by 1% of the time
where the time goes in v6:
time: 47.9 us; the launch traced here: 47.6 us
  Pallas kernels  47 us (98%)
  between operations  0.64 us (1%)
    pallas_call x1, Pallas kernels, local(): pl.pallas_call(functools.partial(fused_kernel, n_cuts, n_coil, inner_cuts...  44 us
    pallas_call x1, Pallas kernels, local(): pl.pallas_call(finish_kernel, out_shape=(jax.ShapeDtypeStruct(flat, f32),...  3.04 us

profile of v6, /device:TPU:0, one launch (start us, length us, event | category | flops | bytes accessed | tf_op | source)
XLA Modules:
  0.0 47.6 jit_solution(17567699297021003642)
XLA Ops:
  0.6 44.0 %back_and_basis.1 = (bf16[96,1024]{1,0:T(8,128)(2,1)}, bf16[96,1024]{1,0:T(8,128)(2,1)}, f32[96,1024]{1,0:T(8,128)}, f32[32,96]{1,0:T(8,128)}) custom-call(s32[8,48]{1,0:T(8,128)} %bitcast.11, bf16[128,128]{1,0:T(8,128)(2,1)} %constant.12.clone.tab_hbm, f32[256,32]{1,0:T(8,128)} %constant.13.clone.rowtab_hbm, bf16[512,256]{1,0:T(8,128)(2,1)} %constant.14.clone.coltab_hbm, ...), custom_call_target="tpu_custom_call" | custom-call | tf_op jit(solution)/shard_map/back_and_basis/pallas_call | solution.py:705
  44.6 3.0 %finish.1 = (f32[8,96,128]{2,1,0:T(8,128)}, f32[8,96,128]{2,1,0:T(8,128)}, f32[32,96]{1,0:T(8,128)}) custom-call(f32[32,96]{1,0:T(8,128)} %get-tuple-element.10.basis_hbm, f32[1,48]{1,0:T(1,128)} %bitcast.12, bf16[96,1024]{1,0:T(8,128)(2,1)} %get-tuple-element.11.high_hbm, bf16[96,1024]{1,0:T(8,128)(2,1)} %get-tuple-element.12.low_hbm, ...), custom_call_target="tpu_custom_call" | custom-call | tf_op jit(solution)/shard_map/finish/pallas_call | solution.py:779

commit v7 on v6

--- a/solution.py
+++ b/solution.py
@@ -607,8 +607,8 @@
     levels = jnp.sum(jnp.where(same, level_ref[...], 0.0), axis=1, keepdims=True)
     for copy in loads[3:]:
         copy.wait()
-    together = math.gcd(rows_here, 4)
-    batch = math.gcd(rows_here, 4)
+    together = math.gcd(rows_here, 8)
+    batch = math.gcd(rows_here, 8)
 
     def send(source, target, first):
         rows = pl.ds(first, batch)
@@ -796,7 +796,7 @@
             pltpu.VMEM(flat, f32),
             pltpu.VMEM(flat, f32),
             dma((7,)),
-            dma((1 + 2 * rows_here // math.gcd(rows_here, 4),)),
+            dma((1 + 2 * (rows_here // math.gcd(rows_here, 8)),)),
         ],
         name="finish",
     )(

time: 47.9 us -> 47.7 us (level)
  no operation moved by 1% of the time
where the time goes in v7:
time: 47.7 us; the launch traced here: 47.4 us
  Pallas kernels  46.8 us (98%)
  between operations  0.64 us (1%)
    pallas_call x1, Pallas kernels, local(): pl.pallas_call(functools.partial(fused_kernel, n_cuts, n_coil, inner_cuts...  44 us
    pallas_call x1, Pallas kernels, local(): pl.pallas_call(finish_kernel, out_shape=(jax.ShapeDtypeStruct(flat, f32),...  2.83 us

profile of v7, /device:TPU:0, one launch (start us, length us, event | category | flops | bytes accessed | tf_op | source)
XLA Modules:
  0.0 47.4 jit_solution(14316625310662534685)
XLA Ops:
  0.6 44.0 %back_and_basis.1 = (bf16[96,1024]{1,0:T(8,128)(2,1)}, bf16[96,1024]{1,0:T(8,128)(2,1)}, f32[96,1024]{1,0:T(8,128)}, f32[32,96]{1,0:T(8,128)}) custom-call(s32[8,48]{1,0:T(8,128)} %bitcast.11, bf16[128,128]{1,0:T(8,128)(2,1)} %constant.12.clone.tab_hbm, f32[256,32]{1,0:T(8,128)} %constant.13.clone.rowtab_hbm, bf16[512,256]{1,0:T(8,128)(2,1)} %constant.14.clone.coltab_hbm, ...), custom_call_target="tpu_custom_call" | custom-call | tf_op jit(solution)/shard_map/back_and_basis/pallas_call | solution.py:705
  44.6 2.8 %finish.1 = (f32[8,96,128]{2,1,0:T(8,128)}, f32[8,96,128]{2,1,0:T(8,128)}, f32[32,96]{1,0:T(8,128)}) custom-call(f32[32,96]{1,0:T(8,128)} %get-tuple-element.10.basis_hbm, f32[1,48]{1,0:T(1,128)} %bitcast.12, bf16[96,1024]{1,0:T(8,128)(2,1)} %get-tuple-element.11.high_hbm, bf16[96,1024]{1,0:T(8,128)(2,1)} %get-tuple-element.12.low_hbm, ...), custom_call_target="tpu_custom_call" | custom-call | tf_op jit(solution)/shard_map/finish/pallas_call | solution.py:779

commit v8 on v6

--- a/solution.py
+++ b/solution.py
@@ -14,7 +14,7 @@
 KX = 256
 BAND = 16
 LANES = 128
-PAIR = 4
+PAIR = 8
 AHEAD = 2
 LATER = 0
 

time: 47.9 us -> 47.2 us (0.985)
  Pallas kernels: 47 us -> 46.3 us
    pallas_call x1, Pallas kernels: 44 us -> 43.3 us  [local(): pl.pallas_call(functools.partial(fused_kernel, n_cuts, n_coil, inner_cuts...]
where the time goes in v8:
time: 47.2 us; the launch traced here: 46.9 us
  Pallas kernels  46.3 us (98%)
  between operations  0.64 us (1%)
    pallas_call x1, Pallas kernels, local(): pl.pallas_call(functools.partial(fused_kernel, n_cuts, n_coil, inner_cuts...  43.3 us
    pallas_call x1, Pallas kernels, local(): pl.pallas_call(finish_kernel, out_shape=(jax.ShapeDtypeStruct(flat, f32),...  3.03 us

profile of v8, /device:TPU:0, one launch (start us, length us, event | category | flops | bytes accessed | tf_op | source)
XLA Modules:
  0.0 46.9 jit_solution(17204043498355767020)
XLA Ops:
  0.6 43.3 %back_and_basis.1 = (bf16[96,1024]{1,0:T(8,128)(2,1)}, bf16[96,1024]{1,0:T(8,128)(2,1)}, f32[96,1024]{1,0:T(8,128)}, f32[32,96]{1,0:T(8,128)}) custom-call(s32[8,48]{1,0:T(8,128)} %bitcast.11, bf16[128,128]{1,0:T(8,128)(2,1)} %constant.12.clone.tab_hbm, f32[256,32]{1,0:T(8,128)} %constant.13.clone.rowtab_hbm, bf16[512,256]{1,0:T(8,128)(2,1)} %constant.14.clone.coltab_hbm, ...), custom_call_target="tpu_custom_call" | custom-call | tf_op jit(solution)/shard_map/back_and_basis/pallas_call | solution.py:705
  43.9 3.0 %finish.1 = (f32[8,96,128]{2,1,0:T(8,128)}, f32[8,96,128]{2,1,0:T(8,128)}, f32[32,96]{1,0:T(8,128)}) custom-call(f32[32,96]{1,0:T(8,128)} %get-tuple-element.10.basis_hbm, f32[1,48]{1,0:T(1,128)} %bitcast.12, bf16[96,1024]{1,0:T(8,128)(2,1)} %get-tuple-element.11.high_hbm, bf16[96,1024]{1,0:T(8,128)(2,1)} %get-tuple-element.12.low_hbm, ...), custom_call_target="tpu_custom_call" | custom-call | tf_op jit(solution)/shard_map/finish/pallas_call | solution.py:779
